TPU v7x, 512 devices: a whole 4x8x8 slice. The times are simulated.
512 devices in a mesh: replica: 4 (over y_hi), fsdp: 16 (over z, core), tensor: 8 (over y_lo, x).
Axes of the slice: x: 4, y: 8 (y_hi: 4, y_lo: 2; y = y_hi * 2 + y_lo), z: 8, core: 2. Of those that a mesh axis runs over, the one named last changes fastest.
Arguments:
- cotangent: bfloat16 [16384, 4096], P(('replica', 'fsdp'), 'tensor'), may hold values from -6 to 6
- gate_pre: bfloat16 [16384, 14336], P(('replica', 'fsdp'), 'tensor'), may hold values from -6 to 6
- up_pre: bfloat16 [16384, 14336], P(('replica', 'fsdp'), 'tensor'), may hold values from -6 to 6
- down_weight: bfloat16 [14336, 4096], P('tensor', 'fsdp'), may hold values from -0.09375 to 0.09375
- projector: bfloat16 [4096, 512], P('tensor', 'fsdp'), may hold values from -0.09375 to 0.09375
Outputs:
- grad_gate: bfloat16 [16384, 14336], P(('replica', 'fsdp'), 'tensor')
- grad_up: bfloat16 [16384, 14336], P(('replica', 'fsdp'), 'tensor')
- projected_grad: float32 [512, 14336], P('fsdp', 'tensor')
All inputs are finite; a program needn't handle non-finite values.
Results may differ from a plain program's by a relative error of at most 0.0049.
Values may be sent and summed in bfloat16 or wider, within the bound.
A program may use at most 64 MiB of HBM per device.

v0:
```python
import math

import jax
import jax.numpy as jnp
from jax import lax
from jax.sharding import PartitionSpec as P


def local(cotangent, gate_pre, up_pre, down_weight, projector):
    whole = lax.all_gather(cotangent, "tensor", axis=1, tiled=True)
    local_rows = cotangent.shape[0]
    hidden_grad = lax.dot_general(
        whole,
        lax.all_gather(down_weight, "fsdp", axis=1, tiled=True),
        (((1,), (1,)), ((), ())),
        preferred_element_type=jnp.float32,
    )
    projector_full_cols = lax.all_gather(projector, "fsdp", axis=1, tiled=True)
    partial_rank = jnp.dot(cotangent, projector_full_cols, preferred_element_type=jnp.float32)
    low_rank = lax.psum(partial_rank, "tensor").astype(jnp.bfloat16)
    gate_float = gate_pre.astype(jnp.float32)
    up_float = up_pre.astype(jnp.float32)
    sigma = jax.nn.sigmoid(gate_float)
    activated = gate_float * sigma
    hidden = (activated * up_float).astype(jnp.bfloat16)
    grad_up = (hidden_grad * activated).astype(jnp.bfloat16)
    grad_gate = (hidden_grad * up_float * sigma * (1.0 + gate_float * (1.0 - sigma))).astype(
        jnp.bfloat16
    )
    replicas = lax.axis_size("replica")
    shards = lax.axis_size("fsdp")
    token_total = local_rows * replicas * shards
    scale_factor = 1.0 / math.sqrt(token_total)
    partial_grad = (
        lax.dot_general(
            low_rank, hidden, (((0,), (0,)), ((), ())), preferred_element_type=jnp.float32
        )
        * scale_factor
    )
    shard_sum = lax.psum_scatter(partial_grad, "fsdp", scatter_dimension=0, tiled=True)
    projected_grad = lax.psum(shard_sum, "replica")
    return (grad_gate, grad_up, projected_grad)


def solution(mesh):
    placed = (
        P(("replica", "fsdp"), "tensor"),
        P(("replica", "fsdp"), "tensor"),
        P(("replica", "fsdp"), "tensor"),
        P("tensor", "fsdp"),
        P("tensor", "fsdp"),
    )
    return jax.shard_map(
        local,
        mesh=mesh,
        in_specs=placed,
        out_specs=(
            P(("replica", "fsdp"), "tensor"),
            P(("replica", "fsdp"), "tensor"),
            P("fsdp", "tensor"),
        ),
        check_vma=False,
    )
```

profile of v0, /device:TPU:1, one launch (start us, length us, event | category | flops | bytes accessed | tf_op | source)
XLA Modules:
  0.0 238.7 jit_solution(15288012159425124146)
XLA Ops:
  8.0 0.0 copy-start.1
  8.0 0.0 copy-start
  8.0 0.0 reduce-scatter.2.cloned.1.call-start
  8.1 26.3 %all_gather.11 = bf16[512,512]{0,1:T(8,128)(2,1)S(1)} all-gather(bf16[512,32]{0,1:T(8,128)(2,1)} %param.9), channel_id=1, replica_groups=mesh['replica'=4,'fsdp'=16,'tensor'=8] {'fsdp'}, dimensions={1}, use_global_device_ids=true | all-gather | bytes 557056 | tf_op jit(solution)/shard_map/all_gather | solution.py:18
  34.4 1.3 fusion.11
  35.6 33.8 %all-reduce.4 = bf16[256,512]{1,0:T(8,128)(2,1)S(1)} all-reduce(f32[256,512]{1,0:T(8,128)S(1)} %fusion.11), channel_id=1, replica_groups=mesh['replica'=4,'fsdp'=16,'tensor'=8] {'tensor'}, use_global_device_ids=true, to_apply=%region_0.0 | all-reduce | flops 131072 | bytes 786432 | tf_op jit(solution)/shard_map/psum | solution.py:20
  69.4 0.0 copy-done.1
  69.4 0.0 copy-done
  69.4 2.8 %convolution_multiply_fusion = f32[512,1792]{1,0:T(8,128)} fusion(bf16[256,1792]{1,0:T(8,128)(2,1)S(1)} %copy-done.1, bf16[256,1792]{1,0:T(8,128)(2,1)S(1)} %copy-done, bf16[256,512]{1,0:T(8,128)(2,1)S(1)} %all-reduce.4), kind=kOutput, calls=%fused_computation | convolution fusion | flops 474349568 | bytes 5767168 | tf_op jit(solution)/shard_map/dot_general | solution.py:35
  72.2 0.0 reduce-scatter.2.cloned.1.call-update
  72.3 0.0 all-gather.3.cloned.1.call-start
  72.3 0.5 all-gather.3.cloned.1.call-update
  72.9 0.0 all-gather.5.cloned.1.call-start
  72.9 0.5 all-gather.5.cloned.1.call-update
  73.4 0.0 all-reduce.3.cloned.1.call-start
  73.5 63.3 %reduce-scatter.2.cloned.1.call-done = f32[32,1792]{1,0:T(8,128)} async-done(((f32[512,1792]{1,0:T(8,128)}), f32[32,1792]{1,0:T(8,128)}) %reduce-scatter.2.cloned.1.call-update) | async-done | bytes 229392 | tf_op jit(solution)/shard_map/reduce_scatter | solution.py:40
  136.8 0.0 all-reduce.3.cloned.1.call-update
  136.8 0.0 all-gather.3.cloned.1.call-done
  136.8 81.2 %all-gather.5.cloned.1.call-done = bf16[1792,4096]{1,0:T(8,128)(2,1)} async-done(((bf16[1792,256]{1,0:T(8,128)(2,1)}), bf16[1792,4096]{1,0:T(8,128)(2,1)}) %all-gather.5.cloned.1.call-update) | async-done | bytes 14680080 | tf_op jit(solution)/shard_map/all_gather | solution.py:14
  218.0 11.6 %multiply_convert_fusion = (bf16[256,1792]{1,0:T(8,128)(2,1)}, bf16[256,1792]{1,0:T(8,128)(2,1)}) fusion(bf16[256,1792]{1,0:T(8,128)(2,1)S(1)} %copy-done, bf16[256,1792]{1,0:T(8,128)(2,1)S(1)} %copy-done.1, bf16[256,4096]{1,0:T(8,128)(2,1)} %all-gather.3.cloned.1.call-done, bf16[1792,4096]{1,0:T(8,128)(2,1)} %all-gather.5.cloned.1.call-done), kind=kOutput, calls=%fused_computation.14 | convolution fusion | flops 3764977664 | bytes 20447232 | tf_op jit(solution)/shard_map/dot_general | solution.py:12
  229.6 0.0 all-reduce.3.cloned.1.call-done
  229.6 1.6 copy.11
Async XLA Ops:
  8.0 61.4 %copy-start.1 = (bf16[256,1792]{1,0:T(8,128)(2,1)S(1)}, bf16[256,1792]{1,0:T(8,128)(2,1)}, u32[]{:S(2)}) copy-start(bf16[256,1792]{1,0:T(8,128)(2,1)} %param.7) | copy-start | bytes 2752516
  8.0 61.4 %copy-start = (bf16[256,1792]{1,0:T(8,128)(2,1)S(1)}, bf16[256,1792]{1,0:T(8,128)(2,1)}, u32[]{:S(2)}) copy-start(bf16[256,1792]{1,0:T(8,128)(2,1)} %param.6) | copy-start | bytes 2752516
  8.0 128.7 %reduce-scatter.2.cloned.1.call-start = ((), (), s32[]{:S(2)}) async-start(), calls=%async_computation.3 | async-start | bytes 3899392 | tf_op jit(solution)/shard_map/reduce_scatter | solution.py:40
  72.3 64.5 %all-gather.3.cloned.1.call-start = ((), (), s32[]{:S(2)}) async-start(), calls=%async_computation.1 | async-start | bytes 2359296 | tf_op jit(solution)/shard_map/all_gather | solution.py:10
  72.9 145.2 %all-gather.5.cloned.1.call-start = ((), (), s32[]{:S(2)}) async-start(), calls=%async_computation.2 | async-start | bytes 15597568 | tf_op jit(solution)/shard_map/all_gather | solution.py:14
  73.4 156.1 %all-reduce.3.cloned.1.call-start = ((), (), s32[]{:S(2)}) async-start(), calls=%async_computation.4 | async-start | bytes 458752 | tf_op jit(solution)/shard_map/psum | solution.py:41
Sparse Core Ops, SparseCore 0:
  72.4 64.3 reduce-scatter.1
  139.7 54.3 all-reduce.2
Sparse Core Ops, SparseCore 1:
  74.8 41.6 all-gather.2
  118.4 99.5 all-gather.4
where the time goes:
time: 239 us
  waiting for transfers between devices  146 us (61%)
  blocking collectives  60.1 us (25%)
  matrix products  15.7 us (7%)
  between operations  15.5 us (6%)
    all_gather x1, waiting for transfers between devices, local(): lax.all_gather(down_weight, 'fsdp', axis=1, tiled=True)  81.2 us
    reduce_scatter x1, waiting for transfers between devices, local(): lax.psum_scatter(partial_grad, 'fsdp', scatter_dimension=0, tiled=True)  63.3 us
    psum x1, blocking collectives, local(): low_rank = lax.psum(partial_rank, 'tensor').astype(jnp.bfloat16)  33.8 us
    all_gather x1, blocking collectives, local(): projector_full_cols = lax.all_gather(projector, 'fsdp', axis=1, tiled=True)  26.3 us
    dot_general x1, matrix products, local(): lax.dot_general(whole, lax.all_gather(down_weight, 'fsdp', axis=1, tiled=...  11.6 us
  transfers between devices with their start and end apart: 4, of which 2 were waited for; matrix products, arithmetic and copies ran while one was open for 5% of the time, Pallas kernels for 0%

commit v1 on v0

v1 whole, which is shorter than its diff:
```python
import functools
import math

import jax
import jax.numpy as jnp
from jax import lax
from jax.experimental import pallas as pl
from jax.experimental.pallas import tpu as pltpu
from jax.sharding import PartitionSpec as P

F32 = jnp.float32
BF16 = jnp.bfloat16
NZ = 8
NX = 4
NT = 8
NR = 4
LAG = 2
SUBS = ((0, 512), (512, 384), (896, 512), (1408, 384))
PLUS = tuple((d, s) for d in (1, 2, 3) for s in range(4)) + ((4, 0), (4, 1))
MINUS = tuple((d, s) for d in (1, 2, 3) for s in range(4)) + ((4, 2), (4, 3))
NM = len(PLUS)
NTILE = 256


def nt_dot(a, b):
    return lax.dot_general(a, b, (((1,), (1,)), ((), ())), preferred_element_type=F32)


def kernel(
    scale, cot_hbm, gate_hbm, up_hbm, w_hbm, pt_hbm, gg_hbm, gu_hbm, pg_hbm,
    wbuf, cotbuf, pbuf, gate, up, act, gfac, hidden, acc,
    lr_part, lr_recv, low_rank, pg, pg_half, pg_sib, ring_send, ring_recv, rep, pg_out,
    local_sem, out_sem, wz_s, wz_r, ws_s, ws_r, p_s, p_r, ps_s, ps_r,
    c_s, c_r, rs_s, rs_r, ag_s, ag_r, x_s, x_r, z_s, z_r, r_s, r_r,
):
    r = lax.axis_index("replica")
    f = lax.axis_index("fsdp")
    t = lax.axis_index("tensor")
    z, c = f // 2, f % 2
    yl, x = t // NX, t % NX

    def zdev(k):
        return {"fsdp": lax.rem(z + k + NZ, NZ) * 2 + c}

    def xdev(k):
        return {"tensor": yl * NX + lax.rem(x + k + NX, NX)}

    sibling = {"fsdp": z * 2 + 1 - c}
    pair = {"tensor": (1 - yl) * NX + x}

    def peer(k):
        return (yl + k // NX) % 2 * NX + (x + k % NX) % NX

    def remote(src, dst, send, recv, device):
        return pltpu.make_async_remote_copy(
            src_ref=src, dst_ref=dst, send_sem=send, recv_sem=recv,
            device_id=device, device_id_type=pl.DeviceIdType.MESH,
        )

    sent = []

    def start(copy):
        copy.start()
        sent.append(copy)

    lanes = pl.ds(pl.multiple_of(c * 256, 256), 256)
    prow = pl.ds(pl.multiple_of(f * 32, 32), 32)
    loads = [
        pltpu.make_async_copy(pt_hbm, pbuf.at[prow, :], local_sem.at[0]),
        pltpu.make_async_copy(w_hbm, wbuf.at[z, :, lanes], local_sem.at[1]),
        pltpu.make_async_copy(cot_hbm, cotbuf.at[t], local_sem.at[2]),
        pltpu.make_async_copy(gate_hbm, gate, local_sem.at[3]),
        pltpu.make_async_copy(up_hbm, up, local_sem.at[4]),
    ]
    for load in loads:
        load.start()

    barrier = pltpu.get_barrier_semaphore()
    greet = [zdev(k) for k in range(1, NZ)] + [sibling]
    greet += [{"tensor": peer(k)} for k in range(1, NT)]
    greet += [{"replica": lax.rem(r + k, NR)} for k in range(1, NR)]
    for device in greet:
        pl.semaphore_signal(
            barrier, inc=1, device_id=device, device_id_type=pl.DeviceIdType.MESH
        )
    pl.semaphore_wait(barrier, len(greet))

    def p_row(zz, cc):
        return pl.ds(pl.multiple_of((zz * 2 + cc) * 32, 32), 32)

    loads[0].wait()
    for k in (1, 7, 2, 6, 3, 5, 4):
        mine = pbuf.at[prow, :]
        start(remote(mine, mine, p_s.at[k - 1], p_r.at[k - 1], zdev(k)))
    start(remote(pbuf.at[prow, :], pbuf.at[prow, :], ps_s.at[0], ps_r.at[0], sibling))

    def w_piece(zz, s, cc):
        at, size = SUBS[s]
        return wbuf.at[
            lax.rem(zz + NZ, NZ), pl.ds(at, size), pl.ds(pl.multiple_of(cc * 256, 256), 256)
        ]

    def w_send(m):
        for sign, messages in ((1, PLUS), (-1, MINUS)):
            d, s = messages[m]
            ref = w_piece(z - sign * (d - 1), s, c)
            way = (1 - sign) // 2
            start(remote(ref, ref, wz_s.at[way, m], wz_r.at[way, m], zdev(sign)))

    def w_event(m):
        for sign, messages in ((1, PLUS), (-1, MINUS)):
            d, s = messages[m]
            ref = w_piece(z - sign * d, s, c)
            way = (1 - sign) // 2
            remote(ref, ref, wz_s.at[way, m], wz_r.at[way, m], zdev(sign)).wait_recv()
        if m + LAG < NM:
            w_send(m + LAG)
        for sign, messages in ((1, PLUS), (-1, MINUS)):
            d, s = messages[m]
            ref = w_piece(z - sign * d, s, c)
            way = (1 - sign) // 2
            start(remote(ref, ref, ws_s.at[way, m], ws_r.at[way, m], sibling))

    def sibling_wait(way, m):
        sign, messages = ((1, PLUS), (-1, MINUS))[way]
        d, s = messages[m]
        ref = w_piece(z - sign * d, s, 1 - c)
        remote(ref, ref, ws_s.at[way, m], ws_r.at[way, m], sibling).wait_recv()

    loads[1].wait()
    for m in range(LAG):
        w_send(m)
    own = wbuf.at[z, :, lanes]
    start(remote(own, own, ws_s.at[0, NM], ws_r.at[0, NM], sibling))

    def chunk(row, xx, half=None):
        at = row * NX + lax.rem(xx + NX, NX)
        if half is None:
            return cotbuf.at[at]
        return cotbuf.at[at, :, pl.ds(half * 256, 256)]

    def c_whole(row, i):
        ref = chunk(row, x)
        start(remote(ref, ref, c_s.at[i, 0], c_r.at[i, 0], xdev(1)))
        start(remote(ref, ref, c_s.at[i, 1], c_r.at[i, 1], xdev(-1)))

    def c_forward(row, i):
        for way, sign in ((0, 1), (1, -1)):
            ref = chunk(row, x - sign)
            remote(ref, ref, c_s.at[i, way], c_r.at[i, way], xdev(sign)).wait_recv()
            ref = chunk(row, x - sign, way)
            start(remote(ref, ref, c_s.at[i, 2 + way], c_r.at[i, 2 + way], xdev(sign)))

    def c_last(row, i):
        for way, sign in ((0, 1), (1, -1)):
            ref = chunk(row, x - 2 * sign, way)
            remote(ref, ref, c_s.at[i, 2 + way], c_r.at[i, 2 + way], xdev(sign)).wait_recv()

    loads[2].wait()
    mine = chunk(yl, x)
    start(remote(mine, mine, c_s.at[2, 0], c_r.at[2, 0], pair))
    c_whole(yl, 0)

    loads[3].wait()
    loads[4].wait()

    def factors(i, carry):
        rows = pl.ds(pl.multiple_of(i * 16, 16), 16)
        g = gate[rows, :].astype(F32)
        u = up[rows, :].astype(F32)
        sigma = jax.nn.sigmoid(g)
        activated = g * sigma
        act[rows, :] = activated
        gfac[rows, :] = u * sigma * (1.0 + g * (1.0 - sigma))
        hidden[rows, :] = (activated * u).astype(BF16)
        return carry

    lax.fori_loop(0, 16, factors, 0)

    ref = chunk(1 - yl, x)
    remote(ref, ref, c_s.at[2, 0], c_r.at[2, 0], pair).wait_recv()
    c_whole(1 - yl, 1)
    c_forward(yl, 0)

    for k in (1, 7, 2, 6, 3, 5, 4):
        zz = lax.rem(z - k + NZ, NZ)
        ref = pbuf.at[p_row(zz, c), :]
        remote(ref, ref, p_s.at[k - 1], p_r.at[k - 1], zdev(k)).wait_recv()
        start(remote(ref, ref, ps_s.at[k], ps_r.at[k], sibling))
    for k in (0, 1, 7, 2, 6, 3, 5, 4):
        ref = pbuf.at[p_row(lax.rem(z - k + NZ, NZ), 1 - c), :]
        remote(ref, ref, ps_s.at[k], ps_r.at[k], sibling).wait_recv()
    lr_part[...] = nt_dot(pbuf[...], cotbuf[t]).reshape(NT, 64, 256)

    w_event(0)
    for k in range(1, NT):
        to = peer(k)
        start(remote(
            lr_part.at[to], lr_recv.at[k - 1], rs_s.at[k - 1], rs_r.at[k - 1], {"tensor": to}
        ))
    c_forward(1 - yl, 1)
    w_event(1)

    total = lr_part[t]
    for k in range(1, NT):
        remote(
            lr_part.at[t], lr_recv.at[k - 1], rs_s.at[k - 1], rs_r.at[k - 1], pair
        ).wait_recv()
        total = total + lr_recv[k - 1]
    low_rank[t] = total.astype(BF16)
    w_event(2)
    for k in range(1, NT):
        ref = low_rank.at[t]
        start(remote(ref, ref, ag_s.at[k - 1], ag_r.at[k - 1], {"tensor": peer(k)}))

    def compute(zz, first=False):
        zz = lax.rem(zz + NZ, NZ)

        def tile(n, carry):
            at = pl.ds(pl.multiple_of(n * NTILE, NTILE), NTILE)
            part = nt_dot(cotbuf[zz], wbuf[zz, at, :])
            acc[:, at] = part if first else acc[:, at] + part
            return carry

        lax.fori_loop(0, 1792 // NTILE, tile, 0)

    c_last(yl, 0)
    c_last(1 - yl, 1)
    ref = wbuf.at[z, :, pl.ds(pl.multiple_of((1 - c) * 256, 256), 256)]
    remote(ref, ref, ws_s.at[0, NM], ws_r.at[0, NM], sibling).wait_recv()
    compute(z, first=True)
    w_event(3)

    for k in range(1, NT):
        back = (yl + k // NX) % 2 * NX + (x - k % NX + NX) % NX
        ref = low_rank.at[back]
        remote(ref, ref, ag_s.at[k - 1], ag_r.at[k - 1], {"tensor": back}).wait_recv()
    lr_all = low_rank[...].reshape(512, 256)

    def grad_tile(n, carry):
        at = pl.ds(pl.multiple_of(n * NTILE, NTILE), NTILE)
        part = jnp.dot(lr_all, hidden[:, at], preferred_element_type=F32)
        part = part.reshape(NZ, 2, 32, NTILE)
        pg[:, :, :, at] = part
        pg_half[:, :, :, at] = part.astype(BF16)
        return carry

    lax.fori_loop(0, 1792 // NTILE, grad_tile, 0)
    w_event(4)
    start(remote(pg_half.at[:, 1 - c], pg_sib, x_s.at[0], x_r.at[0], sibling))
    w_event(5)
    remote(pg_half.at[:, c], pg_sib, x_s.at[0], x_r.at[0], sibling).wait_recv()

    def chip_sum(zz):
        zz = lax.rem(zz + NZ, NZ)
        return pg[zz, c] + pg_sib[zz].astype(F32)

    def ring_wait(way, step):
        sign = 1 - 2 * way
        i = way * 4 + step
        remote(ring_send.at[i], ring_recv.at[i], z_s.at[i], z_r.at[i], zdev(sign)).wait_recv()

    def ring_value(way, step):
        sign = 1 - 2 * way
        reach = 4 - way
        value = chip_sum(z + sign * (reach - step))
        if step > 0:
            ring_wait(way, step - 1)
            value = value + ring_recv[way * 4 + step - 1].astype(F32)
        return value

    def ring_step(step):
        for way in (0, 1):
            if step < 4 - way:
                i = way * 4 + step
                ring_send[i] = ring_value(way, step).astype(BF16)
        for way in (0, 1):
            if step < 4 - way:
                i = way * 4 + step
                start(remote(
                    ring_send.at[i], ring_recv.at[i], z_s.at[i], z_r.at[i], zdev(1 - 2 * way)
                ))

    ring_step(0)

    def shard_compute(d):
        for way in (0, 1):
            for m, (dd, _) in enumerate((PLUS, MINUS)[way]):
                if dd == d:
                    sibling_wait(way, m)
        compute(z - d)
        if d < 4:
            compute(z + d)

    shard_compute(1)
    w_event(6)
    w_event(7)
    ring_step(1)
    shard_compute(2)
    w_event(8)
    w_event(9)
    ring_step(2)
    w_event(10)
    w_event(11)
    ring_step(3)
    shard_compute(3)
    w_event(12)
    ring_wait(1, 2)
    value = chip_sum(z) + ring_recv[6].astype(F32)
    ring_wait(0, 3)
    value = value + ring_recv[3].astype(F32)
    rep[r] = value.astype(BF16)
    w_event(13)
    for k in range(1, NR):
        ref = rep.at[r]
        start(remote(
            ref, ref, r_s.at[k - 1], r_r.at[k - 1], {"replica": lax.rem(r + k, NR)}
        ))
    shard_compute(4)

    outs = []
    for b in range(4):

        def finish(i, carry, b=b):
            rows = pl.ds(pl.multiple_of(b * 64 + i * 16, 16), 16)
            a = acc[rows, :]
            gate[rows, :] = (a * gfac[rows, :]).astype(BF16)
            up[rows, :] = (a * act[rows, :]).astype(BF16)
            return carry

        lax.fori_loop(0, 4, finish, 0)
        rows = pl.ds(b * 64, 64)
        outs.append(pltpu.make_async_copy(gate.at[rows], gg_hbm.at[rows], out_sem.at[2 * b]))
        outs.append(pltpu.make_async_copy(up.at[rows], gu_hbm.at[rows], out_sem.at[2 * b + 1]))
        outs[-2].start()
        outs[-1].start()

    for k in range(1, NR):
        back = lax.rem(r - k + NR, NR)
        ref = rep.at[back]
        remote(ref, ref, r_s.at[k - 1], r_r.at[k - 1], {"replica": back}).wait_recv()
    total = rep[0].astype(F32)
    for k in range(1, NR):
        total = total + rep[k].astype(F32)
    pg_out[...] = total * scale
    last = pltpu.make_async_copy(pg_out, pg_hbm, out_sem.at[8])
    last.start()
    for copy in sent:
        copy.wait_send()
    for copy in outs:
        copy.wait()
    last.wait()


def local(cotangent, gate_pre, up_pre, down_weight, projector):
    rows, width = cotangent.shape
    ff = gate_pre.shape[1]
    tokens = rows * lax.axis_size("replica") * lax.axis_size("fsdp")
    scale = 1.0 / math.sqrt(tokens)
    dma = pltpu.SemaphoreType.DMA
    hbm = pl.BlockSpec(memory_space=pl.ANY)
    return pl.pallas_call(
        functools.partial(kernel, scale),
        out_shape=(
            jax.ShapeDtypeStruct((rows, ff), BF16),
            jax.ShapeDtypeStruct((rows, ff), BF16),
            jax.ShapeDtypeStruct((32, ff), F32),
        ),
        in_specs=[hbm] * 5,
        out_specs=(hbm,) * 3,
        scratch_shapes=[
            pltpu.VMEM((NZ, ff, 512), BF16),
            pltpu.VMEM((NT, rows, width), BF16),
            pltpu.VMEM((512, width), BF16),
            pltpu.VMEM((rows, ff), BF16),
            pltpu.VMEM((rows, ff), BF16),
            pltpu.VMEM((rows, ff), F32),
            pltpu.VMEM((rows, ff), F32),
            pltpu.VMEM((rows, ff), BF16),
            pltpu.VMEM((rows, ff), F32),
            pltpu.VMEM((NT, 64, rows), F32),
            pltpu.VMEM((NT - 1, 64, rows), F32),
            pltpu.VMEM((NT, 64, rows), BF16),
            pltpu.VMEM((NZ, 2, 32, ff), F32),
            pltpu.VMEM((NZ, 2, 32, ff), BF16),
            pltpu.VMEM((NZ, 32, ff), BF16),
            pltpu.VMEM((7, 32, ff), BF16),
            pltpu.VMEM((7, 32, ff), BF16),
            pltpu.VMEM((NR, 32, ff), BF16),
            pltpu.VMEM((32, ff), F32),
            dma((5,)), dma((9,)),
            dma((2, NM)), dma((2, NM)),
            dma((2, NM + 1)), dma((2, NM + 1)),
            dma((7,)), dma((7,)), dma((8,)), dma((8,)),
            dma((3, 4)), dma((3, 4)),
            dma((7,)), dma((7,)), dma((7,)), dma((7,)),
            dma((1,)), dma((1,)), dma((7,)), dma((7,)), dma((3,)), dma((3,)),
        ],
        compiler_params=pltpu.CompilerParams(
            collective_id=0, has_side_effects=True, vmem_limit_bytes=64000 * 1024
        ),
        name="mlp_backward",
    )(cotangent, gate_pre, up_pre, down_weight, projector.T)


def solution(mesh):
    placed = (
        P(("replica", "fsdp"), "tensor"),
        P(("replica", "fsdp"), "tensor"),
        P(("replica", "fsdp"), "tensor"),
        P("tensor", "fsdp"),
        P("tensor", "fsdp"),
    )
    return jax.shard_map(
        local,
        mesh=mesh,
        in_specs=placed,
        out_specs=(
            P(("replica", "fsdp"), "tensor"),
            P(("replica", "fsdp"), "tensor"),
            P("fsdp", "tensor"),
        ),
        check_vma=False,
    )
```

time: 239 us -> 121 us (0.51)
  waiting for transfers between devices: 146 us -> 0 us
  Pallas kernels: 0 us -> 114 us
  blocking collectives: 60.1 us -> 0 us
  matrix products: 15.7 us -> 0 us
  between operations: 15.5 us -> 0.65 us
  local copies, waits for them, and re-layouts: 1.65 us -> 4.11 us
    pallas_call x0 -> x1, Pallas kernels: none -> 114 us  [local(): pl.pallas_call(functools.partial(kernel, scale), out_shape=(jax.ShapeDtyp...]
    all_gather x2 -> x0, waiting for transfers between devices: 81.2 us -> none  [the longest x1 81.2 us: local(): lax.all_gather(down_weight, 'fsdp', axis=1, tiled=True)]
    reduce_scatter x1 -> x0, waiting for transfers between devices: 63.3 us -> none  [local(): lax.psum_scatter(partial_grad, 'fsdp', scatter_dimension=0, tiled=True)]
    psum x1 -> x0, blocking collectives: 33.8 us -> none  [local(): low_rank = lax.psum(partial_rank, 'tensor').astype(jnp.bfloat16)]
    all_gather x1 -> x0, blocking collectives: 26.3 us -> none  [local(): projector_full_cols = lax.all_gather(projector, 'fsdp', axis=1, tiled=True)]
    dot_general x3 -> x0, matrix products: 15.7 us -> none  [the longest x1 11.6 us: local(): lax.dot_general(whole, lax.all_gather(down_weight, 'fsdp', axis=1, tiled=...]
    unnamed x5 -> x7, local copies, waits for them, and re-layouts: 1.65 us -> 4.11 us
  transfers between devices with their start and end apart: 4 -> 0, of which waited for: 2 -> 0; matrix products, arithmetic and copies ran while one was open for 5% -> 0% of each run, Pallas kernels for 0% -> 0%
where the time goes in v1:
time: 121 us; the launch traced here: 119 us
  Pallas kernels  114 us (94%)
  local copies, waits for them, and re-layouts  4.11 us (3%)
    pallas_call x1, Pallas kernels, local(): pl.pallas_call(functools.partial(kernel, scale), out_shape=(jax.ShapeDtyp...  114 us
    unnamed x7, local copies, waits for them, and re-layouts  4.11 us

profile of v1, /device:TPU:1, one launch (start us, length us, event | category | flops | bytes accessed | tf_op | source)
XLA Modules:
  0.0 118.6 jit_solution(5337004081533670718)
XLA Ops:
  0.6 113.9 %mlp_backward.1 = (bf16[256,1792]{1,0:T(8,128)(2,1)}, bf16[256,1792]{1,0:T(8,128)(2,1)}, f32[32,1792]{1,0:T(8,128)}) custom-call(bf16[256,512]{1,0:T(8,128)(2,1)} %cot_hbm.1, bf16[256,1792]{1,0:T(8,128)(2,1)} %gate_hbm.1, bf16[256,1792]{1,0:T(8,128)(2,1)} %up_hbm.1, bf16[1792,256]{1,0:T(8,128)(2,1)} %w_hbm.1, bf16[32,512]{1,0:T(8,128)(2,1)} %bitcast.1), custom_call_target="tpu_custom_call" | custom-call | tf_op jit(solution)/shard_map/mlp_backward/pallas_call | solution.py:362
  114.5 0.0 copy-start
  114.5 2.2 %copy.11 = bf16[256,1792]{1,0:T(8,128)(2,1)} copy(bf16[256,1792]{1,0:T(8,128)(2,1)} %get-tuple-element.6) | data formatting | bytes 1835008
  116.7 0.0 copy-done
  116.7 0.0 copy-start.1
  116.7 0.9 copy.12
  117.7 0.3 copy-done.1
  117.9 0.7 copy.13
Async XLA Ops:
  114.5 2.3 %copy-start = (bf16[256,1792]{1,0:T(8,128)(2,1)S(1)}, bf16[256,1792]{1,0:T(8,128)(2,1)}, u32[]{:S(2)}) copy-start(bf16[256,1792]{1,0:T(8,128)(2,1)} %get-tuple-element.7) | copy-start | bytes 2752516
  116.7 1.2 copy-start.1

commit v2 on v1

--- a/solution.py
+++ b/solution.py
@@ -15,9 +15,15 @@
 NT = 8
 NR = 4
 LAG = 2
-SUBS = ((0, 512), (512, 384), (896, 512), (1408, 384))
-PLUS = tuple((d, s) for d in (1, 2, 3) for s in range(4)) + ((4, 0), (4, 1))
-MINUS = tuple((d, s) for d in (1, 2, 3) for s in range(4)) + ((4, 2), (4, 3))
+HALF = 896
+PHASES = ((0, 512), (512, 384))
+PLUS, MINUS = [], []
+for _phase in range(len(PHASES)):
+    for _d in (1, 2, 3):
+        PLUS += [(_d, _phase, 0), (_d, _phase, 1)]
+        MINUS += [(_d, _phase, 1), (_d, _phase, 0)]
+    PLUS.append((4, _phase, 0))
+    MINUS.append((4, _phase, 1))
 NM = len(PLUS)
 NTILE = 256
 
@@ -28,15 +34,17 @@
 
 def kernel(
     scale, cot_hbm, gate_hbm, up_hbm, w_hbm, pt_hbm, gg_hbm, gu_hbm, pg_hbm,
-    wbuf, cotbuf, pbuf, gate, up, act, gfac, hidden, acc,
-    lr_part, lr_recv, low_rank, pg, pg_half, pg_sib, ring_send, ring_recv, rep, pg_out,
+    wbuf, cotbuf, cot_own, pbuf, gate, up, act, gfac, hidden, acc,
+    hx_send, hx_recv, lr_part, lr_recv, low_rank, pg, pg_half, pg_sib, ring_send, ring_recv, rep, pg_out,
     local_sem, out_sem, wz_s, wz_r, ws_s, ws_r, p_s, p_r, ps_s, ps_r,
     c_s, c_r, rs_s, rs_r, ag_s, ag_r, x_s, x_r, z_s, z_r, r_s, r_r,
+    cr_s, cr_r, h_s, h_r,
 ):
     r = lax.axis_index("replica")
     f = lax.axis_index("fsdp")
     t = lax.axis_index("tensor")
     z, c = f // 2, f % 2
+    par = r % 2
     yl, x = t // NX, t % NX
 
     def zdev(k):
@@ -44,6 +52,9 @@
 
     def xdev(k):
         return {"tensor": yl * NX + lax.rem(x + k + NX, NX)}
+
+    def near(k):
+        return {"replica": lax.rem(r + k + NR, NR)}
 
     sibling = {"fsdp": z * 2 + 1 - c}
     pair = {"tensor": (1 - yl) * NX + x}
@@ -63,14 +74,27 @@
         copy.start()
         sent.append(copy)
 
-    lanes = pl.ds(pl.multiple_of(c * 256, 256), 256)
+    def lane(at):
+        return pl.ds(pl.multiple_of(at, 128), 128)
+
+    lanes = lane(c * 128)
     prow = pl.ds(pl.multiple_of(f * 32, 32), 32)
     loads = [
         pltpu.make_async_copy(pt_hbm, pbuf.at[prow, :], local_sem.at[0]),
-        pltpu.make_async_copy(w_hbm, wbuf.at[z, :, lanes], local_sem.at[1]),
-        pltpu.make_async_copy(cot_hbm, cotbuf.at[t], local_sem.at[2]),
+        pltpu.make_async_copy(
+            w_hbm.at[:, lane(par * 128)], wbuf.at[z, :, lanes], local_sem.at[1]
+        ),
+        pltpu.make_async_copy(cot_hbm, cot_own, local_sem.at[2]),
         pltpu.make_async_copy(gate_hbm, gate, local_sem.at[3]),
         pltpu.make_async_copy(up_hbm, up, local_sem.at[4]),
+    ]
+    loads += [
+        pltpu.make_async_copy(
+            cot_hbm.at[:, lane(q * 256 + par * 128)],
+            cotbuf.at[t, pl.ds(256, 256), pl.ds(q * 128, 128)],
+            local_sem.at[5 + q],
+        )
+        for q in (0, 1)
     ]
     for load in loads:
         load.start()
@@ -94,37 +118,32 @@
         start(remote(mine, mine, p_s.at[k - 1], p_r.at[k - 1], zdev(k)))
     start(remote(pbuf.at[prow, :], pbuf.at[prow, :], ps_s.at[0], ps_r.at[0], sibling))
 
-    def w_piece(zz, s, cc):
-        at, size = SUBS[s]
-        return wbuf.at[
-            lax.rem(zz + NZ, NZ), pl.ds(at, size), pl.ds(pl.multiple_of(cc * 256, 256), 256)
-        ]
+    def w_piece(zz, phase, h, cc):
+        at, size = PHASES[phase]
+        return wbuf.at[lax.rem(zz + NZ, NZ), pl.ds(h * HALF + at, size), lane(cc * 128)]
 
     def w_send(m):
-        for sign, messages in ((1, PLUS), (-1, MINUS)):
-            d, s = messages[m]
-            ref = w_piece(z - sign * (d - 1), s, c)
-            way = (1 - sign) // 2
+        for way, sign, messages in ((0, 1, PLUS), (1, -1, MINUS)):
+            d, phase, h = messages[m]
+            ref = w_piece(z - sign * (d - 1), phase, h, c)
             start(remote(ref, ref, wz_s.at[way, m], wz_r.at[way, m], zdev(sign)))
 
     def w_event(m):
-        for sign, messages in ((1, PLUS), (-1, MINUS)):
-            d, s = messages[m]
-            ref = w_piece(z - sign * d, s, c)
-            way = (1 - sign) // 2
+        for way, sign, messages in ((0, 1, PLUS), (1, -1, MINUS)):
+            d, phase, h = messages[m]
+            ref = w_piece(z - sign * d, phase, h, c)
             remote(ref, ref, wz_s.at[way, m], wz_r.at[way, m], zdev(sign)).wait_recv()
         if m + LAG < NM:
             w_send(m + LAG)
-        for sign, messages in ((1, PLUS), (-1, MINUS)):
-            d, s = messages[m]
-            ref = w_piece(z - sign * d, s, c)
-            way = (1 - sign) // 2
+        for way, sign, messages in ((0, 1, PLUS), (1, -1, MINUS)):
+            d, phase, h = messages[m]
+            ref = w_piece(z - sign * d, phase, h, c)
             start(remote(ref, ref, ws_s.at[way, m], ws_r.at[way, m], sibling))
 
     def sibling_wait(way, m):
         sign, messages = ((1, PLUS), (-1, MINUS))[way]
-        d, s = messages[m]
-        ref = w_piece(z - sign * d, s, 1 - c)
+        d, phase, h = messages[m]
+        ref = w_piece(z - sign * d, phase, h, 1 - c)
         remote(ref, ref, ws_s.at[way, m], ws_r.at[way, m], sibling).wait_recv()
 
     loads[1].wait()
@@ -133,33 +152,57 @@
     own = wbuf.at[z, :, lanes]
     start(remote(own, own, ws_s.at[0, NM], ws_r.at[0, NM], sibling))
 
-    def chunk(row, xx, half=None):
+    def chunk(row, xx, j, half=None):
         at = row * NX + lax.rem(xx + NX, NX)
         if half is None:
-            return cotbuf.at[at]
-        return cotbuf.at[at, :, pl.ds(half * 256, 256)]
-
-    def c_whole(row, i):
-        ref = chunk(row, x)
-        start(remote(ref, ref, c_s.at[i, 0], c_r.at[i, 0], xdev(1)))
-        start(remote(ref, ref, c_s.at[i, 1], c_r.at[i, 1], xdev(-1)))
-
-    def c_forward(row, i):
+            return cotbuf.at[at, pl.ds(j * 256, 256), :]
+        return cotbuf.at[at, pl.ds(j * 256 + half * 128, 128), :]
+
+    def c_whole(row, j, i):
+        ref = chunk(row, x, j)
+        start(remote(ref, ref, c_s.at[i, j, 0], c_r.at[i, j, 0], xdev(1)))
+        start(remote(ref, ref, c_s.at[i, j, 1], c_r.at[i, j, 1], xdev(-1)))
+
+    def c_forward(row, j, i):
         for way, sign in ((0, 1), (1, -1)):
-            ref = chunk(row, x - sign)
-            remote(ref, ref, c_s.at[i, way], c_r.at[i, way], xdev(sign)).wait_recv()
-            ref = chunk(row, x - sign, way)
-            start(remote(ref, ref, c_s.at[i, 2 + way], c_r.at[i, 2 + way], xdev(sign)))
-
-    def c_last(row, i):
+            ref = chunk(row, x - sign, j)
+            remote(ref, ref, c_s.at[i, j, way], c_r.at[i, j, way], xdev(sign)).wait_recv()
+            ref = chunk(row, x - sign, j, way)
+            start(remote(
+                ref, ref, c_s.at[i, j, 2 + way], c_r.at[i, j, 2 + way], xdev(sign)
+            ))
+
+    def c_last(row, j, i):
         for way, sign in ((0, 1), (1, -1)):
-            ref = chunk(row, x - 2 * sign, way)
-            remote(ref, ref, c_s.at[i, 2 + way], c_r.at[i, 2 + way], xdev(sign)).wait_recv()
+            ref = chunk(row, x - 2 * sign, j, way)
+            remote(
+                ref, ref, c_s.at[i, j, 2 + way], c_r.at[i, j, 2 + way], xdev(sign)
+            ).wait_recv()
+
+    def c_pair(j):
+        ref = chunk(yl, x, j)
+        start(remote(ref, ref, c_s.at[2, j, 0], c_r.at[2, j, 0], pair))
+
+    def c_pair_wait(j):
+        ref = chunk(1 - yl, x, j)
+        remote(ref, ref, c_s.at[2, j, 0], c_r.at[2, j, 0], pair).wait_recv()
+
+    def c_replica(way, q):
+        there = 2 - 2 * way
+        return remote(
+            cot_own.at[:, lane(q * 256 + (1 - par) * 128)],
+            cotbuf.at[t, pl.ds(there * 256, 256), pl.ds(q * 128, 128)],
+            cr_s.at[way, q], cr_r.at[way, q], near(1 - 2 * way),
+        )
 
     loads[2].wait()
-    mine = chunk(yl, x)
-    start(remote(mine, mine, c_s.at[2, 0], c_r.at[2, 0], pair))
-    c_whole(yl, 0)
+    for way in (0, 1):
+        for q in (0, 1):
+            start(c_replica(way, q))
+    loads[5].wait()
+    loads[6].wait()
+    c_pair(1)
+    c_whole(yl, 1, 0)
 
     loads[3].wait()
     loads[4].wait()
@@ -177,10 +220,14 @@
 
     lax.fori_loop(0, 16, factors, 0)
 
-    ref = chunk(1 - yl, x)
-    remote(ref, ref, c_s.at[2, 0], c_r.at[2, 0], pair).wait_recv()
-    c_whole(1 - yl, 1)
-    c_forward(yl, 0)
+    c_pair_wait(1)
+    c_whole(1 - yl, 1, 1)
+    c_forward(yl, 1, 0)
+    for j in (0, 2):
+        for q in (0, 1):
+            c_replica(1 - j // 2, q).wait_recv()
+        c_pair(j)
+        c_whole(yl, j, 0)
 
     for k in (1, 7, 2, 6, 3, 5, 4):
         zz = lax.rem(z - k + NZ, NZ)
@@ -190,7 +237,7 @@
     for k in (0, 1, 7, 2, 6, 3, 5, 4):
         ref = pbuf.at[p_row(lax.rem(z - k + NZ, NZ), 1 - c), :]
         remote(ref, ref, ps_s.at[k], ps_r.at[k], sibling).wait_recv()
-    lr_part[...] = nt_dot(pbuf[...], cotbuf[t]).reshape(NT, 64, 256)
+    lr_part[...] = nt_dot(pbuf[...], cot_own[...]).reshape(NT, 64, 256)
 
     w_event(0)
     for k in range(1, NT):
@@ -198,8 +245,13 @@
         start(remote(
             lr_part.at[to], lr_recv.at[k - 1], rs_s.at[k - 1], rs_r.at[k - 1], {"tensor": to}
         ))
-    c_forward(1 - yl, 1)
     w_event(1)
+    c_forward(1 - yl, 1, 1)
+    for j in (0, 2):
+        c_pair_wait(j)
+        c_whole(1 - yl, j, 1)
+        c_forward(yl, j, 0)
+    w_event(2)
 
     total = lr_part[t]
     for k in range(1, NT):
@@ -208,28 +260,29 @@
         ).wait_recv()
         total = total + lr_recv[k - 1]
     low_rank[t] = total.astype(BF16)
-    w_event(2)
     for k in range(1, NT):
         ref = low_rank.at[t]
         start(remote(ref, ref, ag_s.at[k - 1], ag_r.at[k - 1], {"tensor": peer(k)}))
-
-    def compute(zz, first=False):
+    w_event(3)
+    for j in (0, 2):
+        c_forward(1 - yl, j, 1)
+    w_event(4)
+
+    def compute(phase, zz, first=False):
         zz = lax.rem(zz + NZ, NZ)
-
-        def tile(n, carry):
-            at = pl.ds(pl.multiple_of(n * NTILE, NTILE), NTILE)
-            part = nt_dot(cotbuf[zz], wbuf[zz, at, :])
-            acc[:, at] = part if first else acc[:, at] + part
+        at, size = PHASES[phase]
+
+        def part(h, carry):
+            left = cotbuf[zz, pl.ds(pl.multiple_of(h * 256, 256), 512), :]
+            for n in range(0, size, NTILE):
+                width = min(NTILE, size - n)
+                cols = pl.ds(at + n, width)
+                weight = wbuf[zz, pl.ds(pl.multiple_of(h * HALF + at + n, 128), width), :]
+                value = nt_dot(left, weight)
+                acc[h, :, cols] = value if first else acc[h, :, cols] + value
             return carry
 
-        lax.fori_loop(0, 1792 // NTILE, tile, 0)
-
-    c_last(yl, 0)
-    c_last(1 - yl, 1)
-    ref = wbuf.at[z, :, pl.ds(pl.multiple_of((1 - c) * 256, 256), 256)]
-    remote(ref, ref, ws_s.at[0, NM], ws_r.at[0, NM], sibling).wait_recv()
-    compute(z, first=True)
-    w_event(3)
+        lax.fori_loop(0, 2, part, 0)
 
     for k in range(1, NT):
         back = (yl + k // NX) % 2 * NX + (x - k % NX + NX) % NX
@@ -246,9 +299,12 @@
         return carry
 
     lax.fori_loop(0, 1792 // NTILE, grad_tile, 0)
-    w_event(4)
+    w_event(5)
     start(remote(pg_half.at[:, 1 - c], pg_sib, x_s.at[0], x_r.at[0], sibling))
-    w_event(5)
+    for j in range(3):
+        c_last(yl, j, 0)
+        c_last(1 - yl, j, 1)
+    w_event(6)
     remote(pg_half.at[:, c], pg_sib, x_s.at[0], x_r.at[0], sibling).wait_recv()
 
     def chip_sum(zz):
@@ -283,49 +339,86 @@
 
     ring_step(0)
 
-    def shard_compute(d):
+    def shard_compute(phase, d):
+        if d == 0:
+            compute(phase, z, first=True)
+            return
         for way in (0, 1):
-            for m, (dd, _) in enumerate((PLUS, MINUS)[way]):
-                if dd == d:
+            for m, (dd, pp, _) in enumerate((PLUS, MINUS)[way]):
+                if (dd, pp) == (d, phase):
                     sibling_wait(way, m)
-        compute(z - d)
+        compute(phase, z - d)
         if d < 4:
-            compute(z + d)
-
-    shard_compute(1)
-    w_event(6)
+            compute(phase, z + d)
+
+    def hand_over(phase):
+        at, size = PHASES[phase]
+        cols = pl.ds(at, size)
+        for way in (0, 1):
+            for b in range(0, 256, 64):
+                hx_send[way, pl.ds(b, 64), cols] = acc[
+                    way, pl.ds(way * 256 + b, 64), cols
+                ].astype(BF16)
+        for way in (0, 1):
+            start(remote(
+                hx_send.at[way, :, cols], hx_recv.at[way, :, cols],
+                h_s.at[way, phase], h_r.at[way, phase], near(1 - 2 * way),
+            ))
+
+    def hand_over_wait(phase):
+        cols = pl.ds(*PHASES[phase])
+        for way in (0, 1):
+            remote(
+                hx_send.at[way, :, cols], hx_recv.at[way, :, cols],
+                h_s.at[way, phase], h_r.at[way, phase], near(1 - 2 * way),
+            ).wait_recv()
+
+    ref = wbuf.at[z, :, lane((1 - c) * 128)]
+    remote(ref, ref, ws_s.at[0, NM], ws_r.at[0, NM], sibling).wait_recv()
+    shard_compute(0, 0)
     w_event(7)
+    shard_compute(0, 1)
+    w_event(8)
     ring_step(1)
-    shard_compute(2)
-    w_event(8)
+    shard_compute(0, 2)
     w_event(9)
+    shard_compute(0, 3)
+    w_event(10)
     ring_step(2)
-    w_event(10)
+    shard_compute(0, 4)
+    hand_over(0)
     w_event(11)
+    shard_compute(1, 0)
+    shard_compute(1, 1)
+    w_event(12)
     ring_step(3)
-    shard_compute(3)
-    w_event(12)
+    shard_compute(1, 2)
+    w_event(13)
+    shard_compute(1, 3)
+    shard_compute(1, 4)
+    hand_over(1)
     ring_wait(1, 2)
     value = chip_sum(z) + ring_recv[6].astype(F32)
     ring_wait(0, 3)
     value = value + ring_recv[3].astype(F32)
     rep[r] = value.astype(BF16)
-    w_event(13)
     for k in range(1, NR):
         ref = rep.at[r]
-        start(remote(
-            ref, ref, r_s.at[k - 1], r_r.at[k - 1], {"replica": lax.rem(r + k, NR)}
-        ))
-    shard_compute(4)
+        start(remote(ref, ref, r_s.at[k - 1], r_r.at[k - 1], near(k)))
+    hand_over_wait(0)
+    hand_over_wait(1)
 
     outs = []
     for b in range(4):
 
         def finish(i, carry, b=b):
             rows = pl.ds(pl.multiple_of(b * 64 + i * 16, 16), 16)
-            a = acc[rows, :]
-            gate[rows, :] = (a * gfac[rows, :]).astype(BF16)
-            up[rows, :] = (a * act[rows, :]).astype(BF16)
+            for h in (0, 1):
+                cols = pl.ds(h * HALF, HALF)
+                mine = pl.ds(pl.multiple_of((1 - h) * 256 + b * 64 + i * 16, 16), 16)
+                a = acc[h, mine, :] + hx_recv[h, rows, :].astype(F32)
+                gate[rows, cols] = (a * gfac[rows, cols]).astype(BF16)
+                up[rows, cols] = (a * act[rows, cols]).astype(BF16)
             return carry
 
         lax.fori_loop(0, 4, finish, 0)
@@ -369,15 +462,18 @@
         in_specs=[hbm] * 5,
         out_specs=(hbm,) * 3,
         scratch_shapes=[
-            pltpu.VMEM((NZ, ff, 512), BF16),
-            pltpu.VMEM((NT, rows, width), BF16),
+            pltpu.VMEM((NZ, ff, 256), BF16),
+            pltpu.VMEM((NT, 3 * rows, 256), BF16),
+            pltpu.VMEM((rows, width), BF16),
             pltpu.VMEM((512, width), BF16),
             pltpu.VMEM((rows, ff), BF16),
             pltpu.VMEM((rows, ff), BF16),
             pltpu.VMEM((rows, ff), F32),
             pltpu.VMEM((rows, ff), F32),
             pltpu.VMEM((rows, ff), BF16),
-            pltpu.VMEM((rows, ff), F32),
+            pltpu.VMEM((2, 2 * rows, HALF), F32),
+            pltpu.VMEM((2, rows, HALF), BF16),
+            pltpu.VMEM((2, rows, HALF), BF16),
             pltpu.VMEM((NT, 64, rows), F32),
             pltpu.VMEM((NT - 1, 64, rows), F32),
             pltpu.VMEM((NT, 64, rows), BF16),
@@ -388,13 +484,14 @@
             pltpu.VMEM((7, 32, ff), BF16),
             pltpu.VMEM((NR, 32, ff), BF16),
             pltpu.VMEM((32, ff), F32),
-            dma((5,)), dma((9,)),
+            dma((7,)), dma((9,)),
             dma((2, NM)), dma((2, NM)),
             dma((2, NM + 1)), dma((2, NM + 1)),
             dma((7,)), dma((7,)), dma((8,)), dma((8,)),
-            dma((3, 4)), dma((3, 4)),
+            dma((3, 3, 4)), dma((3, 3, 4)),
             dma((7,)), dma((7,)), dma((7,)), dma((7,)),
             dma((1,)), dma((1,)), dma((7,)), dma((7,)), dma((3,)), dma((3,)),
+            dma((2, 2)), dma((2, 2)), dma((2, len(PHASES))), dma((2, len(PHASES))),
         ],
         compiler_params=pltpu.CompilerParams(
             collective_id=0, has_side_effects=True, vmem_limit_bytes=64000 * 1024

time: 121 us -> 117 us (0.967); the launches traced: 119 us -> 116 us
  Pallas kernels: 114 us -> 112 us
    pallas_call x1, Pallas kernels: 114 us -> 112 us  [local(): pl.pallas_call(functools.partial(kernel, scale), out_shape=(jax.ShapeDtyp...]
where the time goes in v2:
time: 117 us; the launch traced here: 116 us
  Pallas kernels  112 us (96%)
  local copies, waits for them, and re-layouts  4.11 us (4%)
    pallas_call x1, Pallas kernels, local(): pl.pallas_call(functools.partial(kernel, scale), out_shape=(jax.ShapeDtyp...  112 us
    unnamed x7, local copies, waits for them, and re-layouts  4.11 us

profile of v2, /device:TPU:1, one launch (start us, length us, event | category | flops | bytes accessed | tf_op | source)
XLA Modules:
  0.0 116.5 jit_solution(3999978427762425455)
XLA Ops:
  0.6 111.7 %mlp_backward.1 = (bf16[256,1792]{1,0:T(8,128)(2,1)}, bf16[256,1792]{1,0:T(8,128)(2,1)}, f32[32,1792]{1,0:T(8,128)}) custom-call(bf16[256,512]{1,0:T(8,128)(2,1)} %cot_hbm.1, bf16[256,1792]{1,0:T(8,128)(2,1)} %gate_hbm.1, bf16[256,1792]{1,0:T(8,128)(2,1)} %up_hbm.1, bf16[1792,256]{1,0:T(8,128)(2,1)} %w_hbm.1, bf16[32,512]{1,0:T(8,128)(2,1)} %bitcast.1), custom_call_target="tpu_custom_call" | custom-call | tf_op jit(solution)/shard_map/mlp_backward/pallas_call | solution.py:455
  112.4 0.0 copy-start
  112.4 2.2 %copy.11 = bf16[256,1792]{1,0:T(8,128)(2,1)} copy(bf16[256,1792]{1,0:T(8,128)(2,1)} %get-tuple-element.6) | data formatting | bytes 1835008
  114.6 0.0 copy-done
  114.6 0.0 copy-start.1
  114.6 0.9 copy.12
  115.6 0.3 copy-done.1
  115.8 0.7 copy.13
Async XLA Ops:
  112.4 2.3 %copy-start = (bf16[256,1792]{1,0:T(8,128)(2,1)S(1)}, bf16[256,1792]{1,0:T(8,128)(2,1)}, u32[]{:S(2)}) copy-start(bf16[256,1792]{1,0:T(8,128)(2,1)} %get-tuple-element.7) | copy-start | bytes 2752516
  114.6 1.2 %copy-start.1 = (f32[32,1792]{1,0:T(8,128)S(1)}, f32[32,1792]{1,0:T(8,128)}, u32[]{:S(2)}) copy-start(f32[32,1792]{1,0:T(8,128)} %get-tuple-element.8) | copy-start | bytes 688132

commit v3 on v0

v3 whole, which is shorter than its diff:
```python
import functools
import math

import jax
import jax.numpy as jnp
from jax import lax
from jax.experimental import pallas as pl
from jax.experimental.pallas import tpu as pltpu
from jax.sharding import PartitionSpec as P

F32 = jnp.float32
BF16 = jnp.bfloat16
NZ = 8
NX = 4
NT = 8
NR = 4
FF = 1792
ROWS = 256
STREAMS = FF // ROWS
HALF = FF // 2
LAG = 3
MESSAGES = sorted(
    ((d, i) for i in range(STREAMS) for d in (1, 2, 3, 4)),
    key=lambda m: (2 * m[1] + 3 * m[0], m[1]),
)
NM = len(MESSAGES)
NEAR_FIRST = (1, 7, 2, 6, 3, 5, 4)


def nt_dot(a, b):
    return lax.dot_general(a, b, (((1,), (1,)), ((), ())), preferred_element_type=F32)


def kernel(
    cot_hbm, gate_hbm, up_hbm, w_hbm, pt_hbm, acc_hbm, hx_hbm, rep_hbm,
    wbuf, cotbuf, cot_own, pbuf, gate, up, hidden, acc, hx,
    lr_part, lr_recv, low_rank, pg, ring_send, ring_recv, rep,
    local_sem, out_sem, wz_s, wz_r, ws_s, ws_r, p_s, p_r, sib_s, sib_r,
    c_s, c_r, cr_s, cr_r, rs_s, rs_r, ag_s, ag_r, z_s, z_r, r_s, r_r, h_s, h_r,
):
    r = lax.axis_index("replica")
    f = lax.axis_index("fsdp")
    t = lax.axis_index("tensor")
    z, c = f // 2, f % 2
    yl, x = t // NX, t % NX
    par = r % 2
    mate = {"replica": lax.rem(r + 1 - 2 * ((r + c) % 2) + NR, NR)}

    def zdev(k):
        return {"fsdp": lax.rem(z + k + NZ, NZ) * 2 + c}

    def xdev(k):
        return {"tensor": yl * NX + lax.rem(x + k + NX, NX)}

    sibling = {"fsdp": z * 2 + 1 - c}
    pair = {"tensor": (1 - yl) * NX + x}

    def peer(k):
        return (yl + k // NX) % 2 * NX + (x + k % NX) % NX

    def peer_back(k):
        return (yl + k // NX) % 2 * NX + (x - k % NX + NX) % NX

    def lane(at, size=128):
        return pl.ds(pl.multiple_of(at, 128), size)

    def rows_at(at, size):
        return pl.ds(pl.multiple_of(at, 32), size)

    def remote(src, dst, send, recv, device):
        return pltpu.make_async_remote_copy(
            src_ref=src, dst_ref=dst, send_sem=send, recv_sem=recv,
            device_id=device, device_id_type=pl.DeviceIdType.MESH,
        )

    sent = []

    def start(copy):
        copy.start()
        sent.append(copy)

    own_w = wbuf.at[:, lane((z * 2 + c) * 128)]
    sib_w = wbuf.at[:, lane((z * 2 + 1 - c) * 128)]
    loads = [
        pltpu.make_async_copy(pt_hbm, pbuf.at[rows_at(z * 32, 32), :], local_sem.at[0]),
        pltpu.make_async_copy(w_hbm.at[:, lane(par * 128)], own_w, local_sem.at[1]),
        pltpu.make_async_copy(cot_hbm, cot_own.at[c], local_sem.at[2]),
        pltpu.make_async_copy(gate_hbm, gate, local_sem.at[3]),
        pltpu.make_async_copy(up_hbm, up, local_sem.at[4]),
    ]
    loads += [
        pltpu.make_async_copy(
            cot_hbm.at[:, lane(q * 256 + par * 128)],
            cotbuf.at[pl.ds(0, ROWS), lane(t * 256 + q * 128)],
            local_sem.at[5 + q],
        )
        for q in (0, 1)
    ]
    for load in loads:
        load.start()

    barrier = pltpu.get_barrier_semaphore()
    greet = [zdev(k) for k in range(1, NZ)] + [sibling]
    greet += [{"tensor": peer(k)} for k in range(1, NT)]
    greet += [{"replica": lax.rem(r + k, NR)} for k in range(1, NR)]
    for device in greet:
        pl.semaphore_signal(
            barrier, inc=1, device_id=device, device_id_type=pl.DeviceIdType.MESH
        )
    pl.semaphore_wait(barrier, len(greet))

    loads[0].wait()
    for k in NEAR_FIRST:
        mine = pbuf.at[rows_at(z * 32, 32), :]
        start(remote(mine, mine, p_s.at[k - 1], p_r.at[k - 1], zdev(k)))

    def chunk(row, xx, j, part=None):
        at = row * NX + lax.rem(xx + NX, NX)
        if part is None:
            return cotbuf.at[pl.ds(j * ROWS, ROWS), lane(at * 256, 256)]
        return cotbuf.at[pl.ds(j * ROWS + part * 128, 128), lane(at * 256, 256)]

    def c_whole(row, j, i):
        ref = chunk(row, x, j)
        for way, sign in ((0, 1), (1, -1)):
            start(remote(ref, ref, c_s.at[i, j, way], c_r.at[i, j, way], xdev(sign)))

    def c_forward(row, j, i):
        for way, sign in ((0, 1), (1, -1)):
            ref = chunk(row, x - sign, j)
            remote(ref, ref, c_s.at[i, j, way], c_r.at[i, j, way], xdev(sign)).wait_recv()
            ref = chunk(row, x - sign, j, way)
            start(remote(
                ref, ref, c_s.at[i, j, 2 + way], c_r.at[i, j, 2 + way], xdev(sign)
            ))

    def c_last(row, j, i):
        for way, sign in ((0, 1), (1, -1)):
            ref = chunk(row, x - 2 * sign, j, way)
            remote(
                ref, ref, c_s.at[i, j, 2 + way], c_r.at[i, j, 2 + way], xdev(sign)
            ).wait_recv()

    def c_pair(j):
        ref = chunk(yl, x, j)
        start(remote(ref, ref, c_s.at[2, j, 0], c_r.at[2, j, 0], pair))

    def c_pair_wait(j):
        ref = chunk(1 - yl, x, j)
        remote(ref, ref, c_s.at[2, j, 0], c_r.at[2, j, 0], pair).wait_recv()

    def c_mate(q):
        return remote(
            cot_own.at[c, :, lane(q * 256 + (1 - par) * 128)],
            cotbuf.at[pl.ds(ROWS, ROWS), lane(t * 256 + q * 128)],
            cr_s.at[q], cr_r.at[q], mate,
        )

    loads[2].wait()
    start(c_mate(0))
    start(c_mate(1))
    loads[5].wait()
    loads[6].wait()
    c_pair(0)
    c_whole(yl, 0, 0)
    start(remote(cot_own.at[c], cot_own.at[c], sib_s.at[0], sib_r.at[0], sibling))

    def w_piece(way, m, zz, cc):
        d, i = MESSAGES[m]
        at, size = (i * ROWS, ROWS) if d < 4 else (i * ROWS + way * 128, 128)
        return wbuf.at[pl.ds(at, size), lane((lax.rem(zz + NZ, NZ) * 2 + cc) * 128)]

    def needs(m):
        d, i = MESSAGES[m]
        return MESSAGES.index((d - 1, i)) if d > 1 else -1

    def w_send(m):
        d = MESSAGES[m][0]
        for way, sign in ((0, 1), (1, -1)):
            ref = w_piece(way, m, z - sign * (d - 1), c)
            start(remote(ref, ref, wz_s.at[way, m], wz_r.at[way, m], zdev(sign)))

    state = {"sent": 0, "event": 0, "ready": False, "todo": []}

    def w_push(done, lag):
        while state["sent"] < min(NM, done + 1 + lag) and needs(state["sent"]) <= done:
            w_send(state["sent"])
            state["sent"] += 1

    def w_event(lag):
        m = state["event"]
        state["event"] += 1
        d, i = MESSAGES[m]
        for way, sign in ((0, 1), (1, -1)):
            ref = w_piece(way, m, z - sign * d, c)
            remote(ref, ref, wz_s.at[way, m], wz_r.at[way, m], zdev(sign)).wait_recv()
        w_push(m, lag)
        for way, sign in ((0, 1), (1, -1)):
            ref = w_piece(way, m, z - sign * d, c)
            start(remote(ref, ref, ws_s.at[way, m], ws_r.at[way, m], sibling))
        if d == 4:
            state["todo"].append(i)

    outs = []

    def compute(i):
        for m, (d, ii) in enumerate(MESSAGES):
            if ii == i:
                for way, sign in ((0, 1), (1, -1)):
                    ref = w_piece(way, m, z - sign * d, 1 - c)
                    remote(ref, ref, ws_s.at[way, m], ws_r.at[way, m], sibling).wait_recv()
        cols = pl.ds(i * ROWS, ROWS)

        def part(j, weight):
            return nt_dot(cotbuf[pl.ds(j * ROWS, ROWS), :], wbuf[cols, :])

        hx[:, cols] = part(1, None).astype(BF16)
        acc[:, cols] = part(0, None)
        start(remote(hx.at[:, cols], hx_hbm.at[:, cols], h_s.at[i], h_r.at[i], mate))
        out = pltpu.make_async_copy(acc.at[:, cols], acc_hbm.at[:, cols], out_sem.at[i])
        out.start()
        outs.append(out)

    def pump(events, lag=LAG):
        for _ in range(events):
            if state["event"] < NM:
                w_event(lag)
            if state["ready"] and len(state["todo"]) > 1:
                compute(state["todo"].pop(0))

    loads[1].wait()
    w_push(-1, LAG)
    start(remote(own_w, own_w, sib_s.at[1], sib_r.at[1], sibling))

    loads[3].wait()
    loads[4].wait()

    def make_hidden(i, carry):
        rows = pl.ds(pl.multiple_of(i * 16, 16), 16)
        g = gate[rows, :].astype(F32)
        activated = g * jax.nn.sigmoid(g)
        hidden[c, rows, :] = (activated * up[rows, :].astype(F32)).astype(BF16)
        return carry

    lax.fori_loop(0, 16, make_hidden, 0)
    c_pair_wait(0)
    c_whole(1 - yl, 0, 1)
    c_forward(yl, 0, 0)
    start(remote(hidden.at[c], hidden.at[c], sib_s.at[2], sib_r.at[2], sibling))

    for k in NEAR_FIRST:
        ref = pbuf.at[rows_at(lax.rem(z - k + NZ, NZ) * 32, 32), :]
        remote(ref, ref, p_s.at[k - 1], p_r.at[k - 1], zdev(k)).wait_recv()
    ref = cot_own.at[1 - c]
    remote(ref, ref, sib_s.at[0], sib_r.at[0], sibling).wait_recv()
    lr_part[...] = nt_dot(pbuf[...], cot_own[...].reshape(2 * ROWS, 512)).reshape(NT, 32, 512)
    pump(1)
    for k in range(1, NT):
        to = peer(k)
        start(remote(
            lr_part.at[to], lr_recv.at[k - 1], rs_s.at[k - 1], rs_r.at[k - 1], {"tensor": to}
        ))
    c_mate(0).wait_recv()
    c_mate(1).wait_recv()
    c_pair(1)
    c_whole(yl, 1, 0)
    pump(1)
    c_forward(1 - yl, 0, 1)
    pump(2)
    total = lr_part[t]
    for k in range(1, NT):
        remote(
            lr_part.at[t], lr_recv.at[k - 1], rs_s.at[k - 1], rs_r.at[k - 1], pair
        ).wait_recv()
        total = total + lr_recv[k - 1]
    low_rank[t] = total.astype(BF16)
    pump(1)
    for k in range(1, NT):
        ref = low_rank.at[t]
        start(remote(ref, ref, ag_s.at[k - 1], ag_r.at[k - 1], {"tensor": peer(k)}))
    c_pair_wait(1)
    c_whole(1 - yl, 1, 1)
    pump(2)
    c_forward(yl, 1, 0)
    pump(2)
    c_forward(1 - yl, 1, 1)
    pump(1)

    for k in range(1, NT):
        ref = low_rank.at[peer_back(k)]
        remote(
            ref, ref, ag_s.at[k - 1], ag_r.at[k - 1], {"tensor": peer_back(k)}
        ).wait_recv()
    ref = hidden.at[1 - c]
    remote(ref, ref, sib_s.at[2], sib_r.at[2], sibling).wait_recv()

    def grad_tile(n, carry):
        at = lane(n * 256, 256)
        both = jnp.concatenate([hidden[0, :, at], hidden[1, :, at]], axis=0)
        part = jnp.dot(
            low_rank[...].reshape(256, 2 * ROWS), both, preferred_element_type=F32
        )
        pg[:, :, at] = part.reshape(NZ, 32, 256)
        return carry

    lax.fori_loop(0, FF // 256, grad_tile, 0)

    def own_part(zz, h):
        return pg[lax.rem(zz + NZ, NZ), :, pl.ds(h * HALF, HALF)]

    def ring(way, step, h):
        i = way * 4 + step
        return remote(
            ring_send.at[h, i], ring_recv.at[h, i], z_s.at[h, i], z_r.at[h, i],
            zdev(1 - 2 * way),
        )

    def ring_step(step, h):
        for way in (0, 1):
            if step < 4 - way:
                i = way * 4 + step
                value = own_part(z + (1 - 2 * way) * (4 - way - step), h)
                if step > 0:
                    ring(way, step - 1, h).wait_recv()
                    value = value + ring_recv[h, i - 1].astype(F32)
                ring_send[h, i] = value.astype(BF16)
        for way in (0, 1):
            if step < 4 - way:
                start(ring(way, step, h))

    def replica_send(h):
        ring(1, 2, h).wait_recv()
        value = own_part(z, h) + ring_recv[h, 6].astype(F32)
        ring(0, 3, h).wait_recv()
        value = value + ring_recv[h, 3].astype(F32)
        rep[h] = value.astype(BF16)
        there = rep_hbm.at[r, :, pl.ds(h * HALF, HALF)]
        for k in range(1, NR):
            start(remote(
                rep.at[h], there, r_s.at[h, k - 1], r_r.at[h, k - 1],
                {"replica": lax.rem(r + k, NR)},
            ))
        out = pltpu.make_async_copy(rep.at[h], there, out_sem.at[STREAMS + h])
        out.start()
        outs.append(out)

    ring_step(0, 0)
    ring_step(0, 1)
    pump(2)
    c_last(yl, 0, 0)
    c_last(1 - yl, 0, 1)
    c_last(yl, 1, 0)
    c_last(1 - yl, 1, 1)
    remote(sib_w, sib_w, sib_s.at[1], sib_r.at[1], sibling).wait_recv()
    state["ready"] = True
    pump(1)
    ring_step(1, 0)
    ring_step(1, 1)
    pump(3)
    ring_step(2, 0)
    ring_step(2, 1)
    pump(3)
    ring_step(3, 0)
    ring_step(3, 1)
    pump(3)
    replica_send(0)
    replica_send(1)
    pump(NM)
    for i in state["todo"]:
        compute(i)

    for i in range(STREAMS):
        cols = pl.ds(i * ROWS, ROWS)
        remote(hx.at[:, cols], hx_hbm.at[:, cols], h_s.at[i], h_r.at[i], mate).wait_recv()
    for h in (0, 1):
        for k in range(1, NR):
            back = lax.rem(r - k + NR, NR)
            remote(
                rep.at[h], rep_hbm.at[back, :, pl.ds(h * HALF, HALF)],
                r_s.at[h, k - 1], r_r.at[h, k - 1], {"replica": back},
            ).wait_recv()
    for copy in sent:
        copy.wait_send()
    for copy in outs:
        copy.wait()


def local(cotangent, gate_pre, up_pre, down_weight, projector):
    rows, width = cotangent.shape
    ff = gate_pre.shape[1]
    tokens = rows * lax.axis_size("replica") * lax.axis_size("fsdp")
    scale = 1.0 / math.sqrt(tokens)
    dma = pltpu.SemaphoreType.DMA
    hbm = pl.BlockSpec(memory_space=pl.ANY)
    own, other, parts = pl.pallas_call(
        kernel,
        out_shape=(
            jax.ShapeDtypeStruct((rows, ff), F32),
            jax.ShapeDtypeStruct((rows, ff), BF16),
            jax.ShapeDtypeStruct((NR, 32, ff), BF16),
        ),
        in_specs=[hbm] * 5,
        out_specs=(hbm,) * 3,
        scratch_shapes=[
            pltpu.VMEM((ff, 2048), BF16),
            pltpu.VMEM((2 * rows, 2048), BF16),
            pltpu.VMEM((2, rows, width), BF16),
            pltpu.VMEM((256, width), BF16),
            pltpu.VMEM((rows, ff), BF16),
            pltpu.VMEM((rows, ff), BF16),
            pltpu.VMEM((2, rows, ff), BF16),
            pltpu.VMEM((rows, ff), F32),
            pltpu.VMEM((rows, ff), BF16),
            pltpu.VMEM((NT, 32, 2 * rows), F32),
            pltpu.VMEM((NT - 1, 32, 2 * rows), F32),
            pltpu.VMEM((NT, 32, 2 * rows), BF16),
            pltpu.VMEM((NZ, 32, ff), F32),
            pltpu.VMEM((2, 7, 32, HALF), BF16),
            pltpu.VMEM((2, 7, 32, HALF), BF16),
            pltpu.VMEM((2, 32, HALF), BF16),
            dma((7,)), dma((STREAMS + 2,)),
            dma((2, NM)), dma((2, NM)), dma((2, NM)), dma((2, NM)),
            dma((7,)), dma((7,)), dma((3,)), dma((3,)),
            dma((3, 2, 4)), dma((3, 2, 4)), dma((2,)), dma((2,)),
            dma((7,)), dma((7,)), dma((7,)), dma((7,)),
            dma((2, 7)), dma((2, 7)), dma((2, 3)), dma((2, 3)),
            dma((STREAMS,)), dma((STREAMS,)),
        ],
        compiler_params=pltpu.CompilerParams(
            collective_id=0, has_side_effects=True, vmem_limit_bytes=56000 * 1024
        ),
        name="mlp_backward",
    )(cotangent, gate_pre, up_pre, down_weight, projector.T)

    hidden_grad = own + other.astype(F32)
    gate_float = gate_pre.astype(F32)
    up_float = up_pre.astype(F32)
    sigma = jax.nn.sigmoid(gate_float)
    grad_up = (hidden_grad * (gate_float * sigma)).astype(BF16)
    grad_gate = (hidden_grad * up_float * sigma * (1.0 + gate_float * (1.0 - sigma))).astype(BF16)
    projected_grad = jnp.sum(parts.astype(F32), axis=0) * scale
    return (grad_gate, grad_up, projected_grad)


def solution(mesh):
    placed = (
        P(("replica", "fsdp"), "tensor"),
        P(("replica", "fsdp"), "tensor"),
        P(("replica", "fsdp"), "tensor"),
        P("tensor", "fsdp"),
        P("tensor", "fsdp"),
    )
    return jax.shard_map(
        local,
        mesh=mesh,
        in_specs=placed,
        out_specs=(
            P(("replica", "fsdp"), "tensor"),
            P(("replica", "fsdp"), "tensor"),
            P("fsdp", "tensor"),
        ),
        check_vma=False,
    )
```

time: 239 us -> 102 us (0.43)
  the two profiles are of different devices: /device:TPU:1 before, /device:TPU:8 now
where the time goes in v3:
time: 102 us; the launch traced here: 101 us
  Pallas kernels  95.9 us (94%)
  other arithmetic  4.79 us (5%)
    pallas_call x1, Pallas kernels, local(): pl.pallas_call(kernel, out_shape=(jax.ShapeDtypeStruct((rows, ff), F32),...  95.9 us
    convert_element_type x1, other arithmetic, local(): grad_up = (hidden_grad * (gate_float * sigma)).astype(BF16)  4.02 us

profile of v3, /device:TPU:8, one launch (start us, length us, event | category | flops | bytes accessed | tf_op | source)
XLA Modules:
  0.0 101.4 jit_solution(6373845589343687739)
XLA Ops:
  0.6 0.0 copy-start.1
  0.6 0.0 copy-start
  0.7 95.9 %mlp_backward.1 = (f32[256,1792]{1,0:T(8,128)}, bf16[256,1792]{1,0:T(8,128)(2,1)}, bf16[4,32,1792]{2,1,0:T(8,128)(2,1)}) custom-call(bf16[256,512]{1,0:T(8,128)(2,1)} %cot_hbm.1, bf16[256,1792]{1,0:T(8,128)(2,1)} %gate_hbm.1, bf16[256,1792]{1,0:T(8,128)(2,1)} %up_hbm.1, bf16[1792,256]{1,0:T(8,128)(2,1)} %w_hbm.1, bf16[32,512]{1,0:T(8,128)(2,1)} %bitcast.1), custom_call_target="tpu_custom_call" | custom-call | tf_op jit(solution)/shard_map/mlp_backward/pallas_call | solution.py:395
  96.6 0.0 copy-done.1
  96.6 0.0 copy-done
  96.6 0.0 copy-start.2
  96.6 4.0 %fusion.7 = (bf16[256,1792]{1,0:T(8,128)(2,1)}, bf16[256,1792]{1,0:T(8,128)(2,1)}) fusion(bf16[256,1792]{1,0:T(8,128)(2,1)S(1)} %copy-done, f32[256,1792]{1,0:T(8,128)} %get-tuple-element.6, bf16[256,1792]{1,0:T(8,128)(2,1)} %get-tuple-element.7, bf16[256,1792]{1,0:T(8,128)(2,1)S(1)} %copy-done.1), kind=kLoop, calls=%fused_computation.10 | loop fusion | flops 7798784 | bytes 6422528 | tf_op jit(solution)/shard_map/convert_element_type | solution.py:439
  100.6 0.0 copy-done.2
  100.6 0.1 convert_reduce_fusion
  100.7 0.7 broadcast_multiply_fusion
Async XLA Ops:
  0.6 95.9 %copy-start.1 = (bf16[256,1792]{1,0:T(8,128)(2,1)S(1)}, bf16[256,1792]{1,0:T(8,128)(2,1)}, u32[]{:S(2)}) copy-start(bf16[256,1792]{1,0:T(8,128)(2,1)} %up_hbm.1) | copy-start | bytes 2752516
  0.6 95.9 %copy-start = (bf16[256,1792]{1,0:T(8,128)(2,1)S(1)}, bf16[256,1792]{1,0:T(8,128)(2,1)}, u32[]{:S(2)}) copy-start(bf16[256,1792]{1,0:T(8,128)(2,1)} %gate_hbm.1) | copy-start | bytes 2752516
  96.6 4.0 %copy-start.2 = (bf16[4,32,1792]{2,1,0:T(8,128)(2,1)S(1)}, bf16[4,32,1792]{2,1,0:T(8,128)(2,1)}, u32[]{:S(2)}) copy-start(bf16[4,32,1792]{2,1,0:T(8,128)(2,1)} %get-tuple-element.8) | copy-start | bytes 1376260

commit v4 on v3

v4 whole, which is shorter than its diff:
```python
import functools
import math

import jax
import jax.numpy as jnp
from jax import lax
from jax.experimental import pallas as pl
from jax.experimental.pallas import tpu as pltpu
from jax.sharding import PartitionSpec as P

F32 = jnp.float32
BF16 = jnp.bfloat16
NZ = 8
NX = 4
NT = 8
NR = 4
FF = 1792
ROWS = 256
STREAMS = FF // ROWS
HALF = FF // 2
LAG = 5
MESSAGES = sorted(
    ((d, i) for i in range(STREAMS) for d in (1, 2, 3, 4)),
    key=lambda m: (2 * m[1] + 3 * m[0], m[1]),
)
NM = len(MESSAGES)
NEAR_FIRST = (1, 7, 2, 6, 3, 5, 4)


def nt_dot(a, b):
    return lax.dot_general(a, b, (((1,), (1,)), ((), ())), preferred_element_type=F32)


def kernel(
    cot_hbm, gate_hbm, up_hbm, w_hbm, pt_hbm, acc_hbm, hx_hbm, rep_hbm,
    wbuf, cotbuf, cot_own, pbuf, gate, up, hidden, acc, hx,
    lr_part, lr_recv, low_rank, pg, ring_send, ring_recv, rep,
    local_sem, out_sem, wz_s, wz_r, ws_s, ws_r, p_s, p_r, sib_s, sib_r,
    own_s, own_r, c_s, c_r, cr_s, cr_r, rs_s, rs_r, ag_s, ag_r, z_s, z_r, r_s, r_r, h_s, h_r,
):
    r = lax.axis_index("replica")
    f = lax.axis_index("fsdp")
    t = lax.axis_index("tensor")
    z, c = f // 2, f % 2
    yl, x = t // NX, t % NX
    par = r % 2
    mate = {"replica": lax.rem(r + 1 - 2 * ((r + c) % 2) + NR, NR)}

    def zdev(k, core=c):
        return {"fsdp": lax.rem(z + k + NZ, NZ) * 2 + core}

    def xdev(k):
        return {"tensor": yl * NX + lax.rem(x + k + NX, NX)}

    sibling = {"fsdp": z * 2 + 1 - c}
    pair = {"tensor": (1 - yl) * NX + x}

    def peer(k):
        return (yl + k // NX) % 2 * NX + (x + k % NX) % NX

    def peer_back(k):
        return (yl + k // NX) % 2 * NX + (x - k % NX + NX) % NX

    def lane(at, size=128):
        return pl.ds(pl.multiple_of(at, 128), size)

    def rows_at(at, size):
        return pl.ds(pl.multiple_of(at, 32), size)

    def remote(src, dst, send, recv, device):
        return pltpu.make_async_remote_copy(
            src_ref=src, dst_ref=dst, send_sem=send, recv_sem=recv,
            device_id=device, device_id_type=pl.DeviceIdType.MESH,
        )

    sent, outs = [], []

    def start(copy):
        copy.start()
        sent.append(copy)

    own_w = wbuf.at[:, lane((z * 2 + c) * 128)]
    loads = [
        pltpu.make_async_copy(pt_hbm, pbuf.at[rows_at(f * 32, 32), :], local_sem.at[0]),
        pltpu.make_async_copy(w_hbm.at[:, lane(par * 128)], own_w, local_sem.at[1]),
        pltpu.make_async_copy(cot_hbm, cot_own.at[c], local_sem.at[2]),
        pltpu.make_async_copy(gate_hbm, gate, local_sem.at[3]),
        pltpu.make_async_copy(up_hbm, up, local_sem.at[4]),
    ]
    loads += [
        pltpu.make_async_copy(
            cot_hbm.at[:, lane(q * 256 + par * 128)],
            cotbuf.at[pl.ds(0, ROWS), lane(t * 256 + q * 128)],
            local_sem.at[5 + q],
        )
        for q in (0, 1)
    ]
    for load in loads:
        load.start()

    barrier = pltpu.get_barrier_semaphore()
    greet = [zdev(k) for k in range(1, NZ)] + [zdev(k, 1 - c) for k in range(NZ)]
    greet += [{"tensor": peer(k)} for k in range(1, NT)]
    greet += [{"replica": lax.rem(r + k, NR)} for k in range(1, NR)]
    greet += [{"replica": lax.rem(r + k, NR), **sibling} for k in range(1, NR)]
    for device in greet:
        pl.semaphore_signal(
            barrier, inc=1, device_id=device, device_id_type=pl.DeviceIdType.MESH
        )
    pl.semaphore_wait(barrier, len(greet))

    def p_copy(core, k, zz):
        ref = pbuf.at[rows_at((zz * 2 + core) * 32, 32), :]
        return remote(ref, ref, p_s.at[core, k], p_r.at[core, k], zdev(k, 1))

    def p_send(core):
        loads[0].wait()
        for k in NEAR_FIRST:
            start(p_copy(core, k, z))
        if core == 0:
            start(p_copy(core, 0, z))

    def chunk(row, xx, j, part=None):
        at = row * NX + lax.rem(xx + NX, NX)
        if part is None:
            return cotbuf.at[pl.ds(j * ROWS, ROWS), lane(at * 256, 256)]
        return cotbuf.at[pl.ds(j * ROWS + part * 128, 128), lane(at * 256, 256)]

    def c_whole(row, j, i):
        ref = chunk(row, x, j)
        for way, sign in ((0, 1), (1, -1)):
            start(remote(ref, ref, c_s.at[i, j, way], c_r.at[i, j, way], xdev(sign)))

    def c_forward(row, j, i):
        for way, sign in ((0, 1), (1, -1)):
            ref = chunk(row, x - sign, j)
            remote(ref, ref, c_s.at[i, j, way], c_r.at[i, j, way], xdev(sign)).wait_recv()
            ref = chunk(row, x - sign, j, way)
            start(remote(
                ref, ref, c_s.at[i, j, 2 + way], c_r.at[i, j, 2 + way], xdev(sign)
            ))

    def c_last(row, j, i):
        for way, sign in ((0, 1), (1, -1)):
            ref = chunk(row, x - 2 * sign, j, way)
            remote(
                ref, ref, c_s.at[i, j, 2 + way], c_r.at[i, j, 2 + way], xdev(sign)
            ).wait_recv()

    def c_pair(j):
        ref = chunk(yl, x, j)
        start(remote(ref, ref, c_s.at[2, j, 0], c_r.at[2, j, 0], pair))

    def c_pair_wait(j):
        ref = chunk(1 - yl, x, j)
        remote(ref, ref, c_s.at[2, j, 0], c_r.at[2, j, 0], pair).wait_recv()

    def c_mate(q):
        return remote(
            cot_own.at[c, :, lane(q * 256 + (1 - par) * 128)],
            cotbuf.at[pl.ds(ROWS, ROWS), lane(t * 256 + q * 128)],
            cr_s.at[q], cr_r.at[q], mate,
        )

    def c_begin():
        loads[2].wait()
        start(c_mate(0))
        start(c_mate(1))
        loads[5].wait()
        loads[6].wait()
        c_pair(0)
        c_whole(yl, 0, 0)

    def w_piece(way, m, zz):
        d, i = MESSAGES[m]
        at, size = (i * ROWS, ROWS) if d < 4 else (i * ROWS + way * 128, 128)
        return wbuf.at[pl.ds(at, size), lane(lax.rem(zz + NZ, NZ) * 256, 256)]

    def w_own(i, core):
        ref = wbuf.at[pl.ds(i * ROWS, ROWS), lane((z * 2 + core) * 128)]
        return remote(ref, ref, own_s.at[core, i], own_r.at[core, i], sibling)

    def needs(m):
        d, i = MESSAGES[m]
        return MESSAGES.index((d - 1, i)) if d > 1 else -1

    def w_send(m):
        d, i = MESSAGES[m]
        if d == 1:
            w_own(i, 1).wait_recv()
        for way, sign in ((0, 1), (1, -1)):
            ref = w_piece(way, m, z - sign * (d - 1))
            start(remote(ref, ref, wz_s.at[way, m], wz_r.at[way, m], zdev(sign)))

    def w_pass(way, m):
        sign = 1 - 2 * way
        ref = w_piece(way, m, z - sign * MESSAGES[m][0])
        return remote(ref, ref, ws_s.at[way, m], ws_r.at[way, m], sibling)

    state = {"sent": 0, "event": 0, "ready": False, "todo": []}

    def w_push(done, lag):
        while state["sent"] < min(NM, done + 1 + lag) and needs(state["sent"]) <= done:
            w_send(state["sent"])
            state["sent"] += 1

    def w_event(lag):
        m = state["event"]
        state["event"] += 1
        d, i = MESSAGES[m]
        for way, sign in ((0, 1), (1, -1)):
            ref = w_piece(way, m, z - sign * d)
            remote(ref, ref, wz_s.at[way, m], wz_r.at[way, m], zdev(sign)).wait_recv()
        w_push(m, lag)
        start(w_pass(0, m))
        start(w_pass(1, m))
        if d == 4:
            state["todo"].append(i)

    def compute(i, core):
        if core == 1:
            w_own(i, 0).wait_recv()
            for m, (_, ii) in enumerate(MESSAGES):
                if ii == i:
                    w_pass(0, m).wait_recv()
                    w_pass(1, m).wait_recv()
        cols = pl.ds(i * ROWS, ROWS)

        def part(j):
            return nt_dot(cotbuf[pl.ds(j * ROWS, ROWS), :], wbuf[cols, :])

        hx[:, cols] = part(1).astype(BF16)
        acc[:, cols] = part(0)
        start(remote(hx.at[:, cols], hx_hbm.at[:, cols], h_s.at[i], h_r.at[i], mate))
        out = pltpu.make_async_copy(acc.at[:, cols], acc_hbm.at[:, cols], out_sem.at[i])
        out.start()
        outs.append(out)

    def pump(events, lag=LAG):
        for _ in range(events):
            if state["event"] < NM:
                w_event(lag)
            if state["ready"] and state["todo"]:
                compute(state["todo"].pop(0), 0)

    def make_hidden(i, carry):
        rows = pl.ds(pl.multiple_of(i * 16, 16), 16)
        g = gate[rows, :].astype(F32)
        activated = g * jax.nn.sigmoid(g)
        hidden[c, rows, :] = (activated * up[rows, :].astype(F32)).astype(BF16)
        return carry

    def hidden_now():
        loads[3].wait()
        loads[4].wait()
        lax.fori_loop(0, 16, make_hidden, 0)

    def to_second(ref, i):
        return remote(ref, ref, sib_s.at[i], sib_r.at[i], sibling)

    def low_rank_part():
        for k in NEAR_FIRST:
            p_copy(0, k, lax.rem(z - k + NZ, NZ)).wait_recv()
            p_copy(1, k, lax.rem(z - k + NZ, NZ)).wait_recv()
        p_copy(0, 0, z).wait_recv()
        to_second(cot_own.at[0], 0).wait_recv()
        part = nt_dot(pbuf[...], cot_own[...].reshape(2 * ROWS, 512))
        lr_part[...] = part.reshape(NT, 64, 2 * ROWS)

    def low_rank_scatter():
        for k in range(1, NT):
            to = peer(k)
            start(remote(
                lr_part.at[to], lr_recv.at[k - 1], rs_s.at[k - 1], rs_r.at[k - 1],
                {"tensor": to},
            ))

    def low_rank_sum():
        total = lr_part[t]
        for k in range(1, NT):
            remote(
                lr_part.at[t], lr_recv.at[k - 1], rs_s.at[k - 1], rs_r.at[k - 1], pair
            ).wait_recv()
            total = total + lr_recv[k - 1]
        low_rank[t] = total.astype(BF16)

    def low_rank_gather():
        for k in range(1, NT):
            ref = low_rank.at[t]
            start(remote(
                ref, ref, ag_s.at[k - 1], ag_r.at[k - 1], {"tensor": peer(k)}
            ))

    def low_rank_wait():
        for k in range(1, NT):
            ref = low_rank.at[peer_back(k)]
            remote(
                ref, ref, ag_s.at[k - 1], ag_r.at[k - 1], {"tensor": peer_back(k)}
            ).wait_recv()

    def grad_tile(n, carry):
        at = lane(n * 256, 256)
        both = jnp.concatenate([hidden[0, :, at], hidden[1, :, at]], axis=0)
        part = jnp.dot(
            low_rank[...].reshape(512, 2 * ROWS), both, preferred_element_type=F32
        )
        pg[:, :, at] = part.reshape(NZ, 64, 256)
        return carry

    def own_part(zz, h):
        return pg[lax.rem(zz + NZ, NZ), :, pl.ds(h * HALF, HALF)]

    def ring(way, step, h):
        i = way * 4 + step
        return remote(
            ring_send.at[h, i], ring_recv.at[h, i], z_s.at[h, i], z_r.at[h, i],
            zdev(1 - 2 * way),
        )

    def ring_step(step, h):
        for way in (0, 1):
            if step < 4 - way:
                i = way * 4 + step
                value = own_part(z + (1 - 2 * way) * (4 - way - step), h)
                if step > 0:
                    ring(way, step - 1, h).wait_recv()
                    value = value + ring_recv[h, i - 1].astype(F32)
                ring_send[h, i] = value.astype(BF16)
        for way in (0, 1):
            if step < 4 - way:
                start(ring(way, step, h))

    def replica_send(h):
        ring(1, 2, h).wait_recv()
        value = own_part(z, h) + ring_recv[h, 6].astype(F32)
        ring(0, 3, h).wait_recv()
        value = value + ring_recv[h, 3].astype(F32)
        rep[h] = value.astype(BF16)
        there = rep_hbm.at[r, :, pl.ds(h * HALF, HALF)]
        for k in range(NR):
            for core in (0, 1):
                mine = rep.at[h, pl.ds(core * 32, 32), :]
                if (k, core) == (0, 1):
                    out = pltpu.make_async_copy(mine, there, out_sem.at[STREAMS + h])
                    out.start()
                    outs.append(out)
                else:
                    start(remote(
                        mine, there, r_s.at[core, h, k], r_r.at[core, h, k],
                        {"replica": lax.rem(r + k, NR), "fsdp": z * 2 + core},
                    ))

    def finish(core):
        for i in range(STREAMS):
            cols = pl.ds(i * ROWS, ROWS)
            remote(
                hx.at[:, cols], hx_hbm.at[:, cols], h_s.at[i], h_r.at[i], mate
            ).wait_recv()
        for h in (0, 1):
            for k in range(core, NR):
                back = lax.rem(r - k + NR, NR)
                remote(
                    rep.at[h, pl.ds(0, 32), :], rep_hbm.at[back, :, pl.ds(h * HALF, HALF)],
                    r_s.at[core, h, k], r_r.at[core, h, k], sibling,
                ).wait_recv()
        for copy in sent:
            copy.wait_send()
        for copy in outs:
            copy.wait()
        sent.clear()
        outs.clear()

    @pl.when(c == 0)
    def _():
        p_send(0)
        loads[1].wait()
        w_push(-1, LAG)
        c_begin()
        start(to_second(cot_own.at[0], 0))
        for i in range(STREAMS):
            start(w_own(i, 0))
        hidden_now()
        start(to_second(hidden.at[0], 1))
        c_pair_wait(0)
        c_whole(1 - yl, 0, 1)
        c_forward(yl, 0, 0)
        pump(1)
        c_mate(0).wait_recv()
        c_mate(1).wait_recv()
        c_pair(1)
        c_whole(yl, 1, 0)
        pump(1)
        c_forward(1 - yl, 0, 1)
        pump(2)
        c_pair_wait(1)
        c_whole(1 - yl, 1, 1)
        c_forward(yl, 1, 0)
        pump(4)
        c_forward(1 - yl, 1, 1)
        pump(2)
        c_last(yl, 0, 0)
        c_last(1 - yl, 0, 1)
        c_last(yl, 1, 0)
        c_last(1 - yl, 1, 1)
        state["ready"] = True
        pump(NM)
        for i in state["todo"]:
            compute(i, 0)
        finish(0)

    @pl.when(c == 1)
    def _():
        loads[1].wait()
        for i in range(STREAMS):
            start(w_own(i, 1))
        p_send(1)
        c_begin()
        hidden_now()
        c_pair_wait(0)
        c_whole(1 - yl, 0, 1)
        c_forward(yl, 0, 0)
        low_rank_part()
        low_rank_scatter()
        c_mate(0).wait_recv()
        c_mate(1).wait_recv()
        c_pair(1)
        c_whole(yl, 1, 0)
        c_forward(1 - yl, 0, 1)
        low_rank_sum()
        low_rank_gather()
        c_pair_wait(1)
        c_whole(1 - yl, 1, 1)
        c_forward(yl, 1, 0)
        low_rank_wait()
        to_second(hidden.at[0], 1).wait_recv()
        lax.fori_loop(0, FF // 256, grad_tile, 0)
        ring_step(0, 0)
        ring_step(0, 1)
        c_forward(1 - yl, 1, 1)
        ring_step(1, 0)
        ring_step(1, 1)
        c_last(yl, 0, 0)
        c_last(1 - yl, 0, 1)
        c_last(yl, 1, 0)
        c_last(1 - yl, 1, 1)
        compute(0, 1)
        ring_step(2, 0)
        ring_step(2, 1)
        compute(1, 1)
        ring_step(3, 0)
        ring_step(3, 1)
        compute(2, 1)
        replica_send(0)
        replica_send(1)
        for i in range(3, STREAMS):
            compute(i, 1)
        finish(1)


def local(cotangent, gate_pre, up_pre, down_weight, projector):
    rows, width = cotangent.shape
    ff = gate_pre.shape[1]
    tokens = rows * lax.axis_size("replica") * lax.axis_size("fsdp")
    scale = 1.0 / math.sqrt(tokens)
    dma = pltpu.SemaphoreType.DMA
    hbm = pl.BlockSpec(memory_space=pl.ANY)
    own, other, parts = pl.pallas_call(
        kernel,
        out_shape=(
            jax.ShapeDtypeStruct((rows, ff), F32),
            jax.ShapeDtypeStruct((rows, ff), BF16),
            jax.ShapeDtypeStruct((NR, 32, ff), BF16),
        ),
        in_specs=[hbm] * 5,
        out_specs=(hbm,) * 3,
        scratch_shapes=[
            pltpu.VMEM((ff, 2048), BF16),
            pltpu.VMEM((2 * rows, 2048), BF16),
            pltpu.VMEM((2, rows, width), BF16),
            pltpu.VMEM((512, width), BF16),
            pltpu.VMEM((rows, ff), BF16),
            pltpu.VMEM((rows, ff), BF16),
            pltpu.VMEM((2, rows, ff), BF16),
            pltpu.VMEM((rows, ff), F32),
            pltpu.VMEM((rows, ff), BF16),
            pltpu.VMEM((NT, 64, 2 * rows), F32),
            pltpu.VMEM((NT - 1, 64, 2 * rows), F32),
            pltpu.VMEM((NT, 64, 2 * rows), BF16),
            pltpu.VMEM((NZ, 64, ff), F32),
            pltpu.VMEM((2, 7, 64, HALF), BF16),
            pltpu.VMEM((2, 7, 64, HALF), BF16),
            pltpu.VMEM((2, 64, HALF), BF16),
            dma((7,)), dma((STREAMS + 2,)),
            dma((2, NM)), dma((2, NM)), dma((2, NM)), dma((2, NM)),
            dma((2, NZ)), dma((2, NZ)), dma((2,)), dma((2,)),
            dma((2, STREAMS)), dma((2, STREAMS)),
            dma((3, 2, 4)), dma((3, 2, 4)), dma((2,)), dma((2,)),
            dma((7,)), dma((7,)), dma((7,)), dma((7,)),
            dma((2, 7)), dma((2, 7)), dma((2, 2, NR)), dma((2, 2, NR)),
            dma((STREAMS,)), dma((STREAMS,)),
        ],
        compiler_params=pltpu.CompilerParams(
            collective_id=0, has_side_effects=True, vmem_limit_bytes=56000 * 1024
        ),
        name="mlp_backward",
    )(cotangent, gate_pre, up_pre, down_weight, projector.T)

    hidden_grad = own + other.astype(F32)
    gate_float = gate_pre.astype(F32)
    up_float = up_pre.astype(F32)
    sigma = jax.nn.sigmoid(gate_float)
    grad_up = (hidden_grad * (gate_float * sigma)).astype(BF16)
    grad_gate = (hidden_grad * up_float * sigma * (1.0 + gate_float * (1.0 - sigma))).astype(BF16)
    projected_grad = jnp.sum(parts.astype(F32), axis=0) * scale
    return (grad_gate, grad_up, projected_grad)


def solution(mesh):
    placed = (
        P(("replica", "fsdp"), "tensor"),
        P(("replica", "fsdp"), "tensor"),
        P(("replica", "fsdp"), "tensor"),
        P("tensor", "fsdp"),
        P("tensor", "fsdp"),
    )
    return jax.shard_map(
        local,
        mesh=mesh,
        in_specs=placed,
        out_specs=(
            P(("replica", "fsdp"), "tensor"),
            P(("replica", "fsdp"), "tensor"),
            P("fsdp", "tensor"),
        ),
        check_vma=False,
    )
```

time: 102 us -> 99.7 us (0.977)
  the two profiles are of different devices: /device:TPU:8 before, /device:TPU:1 now
where the time goes in v4:
time: 99.7 us; the launch traced here: 99 us
  Pallas kernels  93.6 us (94%)
  other arithmetic  4.79 us (5%)
    pallas_call x1, Pallas kernels, local(): pl.pallas_call(kernel, out_shape=(jax.ShapeDtypeStruct((rows, ff), F32),...  93.6 us
    convert_element_type x1, other arithmetic, local(): grad_up = (hidden_grad * (gate_float * sigma)).astype(BF16)  4.02 us

profile of v4, /device:TPU:1, one launch (start us, length us, event | category | flops | bytes accessed | tf_op | source)
XLA Modules:
  0.0 99.0 jit_solution(12903869452810185587)
XLA Ops:
  0.6 0.0 copy-start.1
  0.6 0.0 copy-start
  0.7 93.6 %mlp_backward.1 = (f32[256,1792]{1,0:T(8,128)}, bf16[256,1792]{1,0:T(8,128)(2,1)}, bf16[4,32,1792]{2,1,0:T(8,128)(2,1)}) custom-call(bf16[256,512]{1,0:T(8,128)(2,1)} %cot_hbm.1, bf16[256,1792]{1,0:T(8,128)(2,1)} %gate_hbm.1, bf16[256,1792]{1,0:T(8,128)(2,1)} %up_hbm.1, bf16[1792,256]{1,0:T(8,128)(2,1)} %w_hbm.1, bf16[32,512]{1,0:T(8,128)(2,1)} %bitcast.1), custom_call_target="tpu_custom_call" | custom-call | tf_op jit(solution)/shard_map/mlp_backward/pallas_call | solution.py:467
  94.2 0.0 copy-done.1
  94.2 0.0 copy-done
  94.2 0.0 copy-start.2
  94.2 4.0 %fusion.7 = (bf16[256,1792]{1,0:T(8,128)(2,1)}, bf16[256,1792]{1,0:T(8,128)(2,1)}) fusion(bf16[256,1792]{1,0:T(8,128)(2,1)S(1)} %copy-done, f32[256,1792]{1,0:T(8,128)} %get-tuple-element.6, bf16[256,1792]{1,0:T(8,128)(2,1)} %get-tuple-element.7, bf16[256,1792]{1,0:T(8,128)(2,1)S(1)} %copy-done.1), kind=kLoop, calls=%fused_computation.10 | loop fusion | flops 7798784 | bytes 6422528 | tf_op jit(solution)/shard_map/convert_element_type | solution.py:512
  98.3 0.0 copy-done.2
  98.3 0.1 convert_reduce_fusion
  98.3 0.7 broadcast_multiply_fusion
Async XLA Ops:
  0.6 93.6 %copy-start.1 = (bf16[256,1792]{1,0:T(8,128)(2,1)S(1)}, bf16[256,1792]{1,0:T(8,128)(2,1)}, u32[]{:S(2)}) copy-start(bf16[256,1792]{1,0:T(8,128)(2,1)} %up_hbm.1) | copy-start | bytes 2752516
  0.6 93.6 %copy-start = (bf16[256,1792]{1,0:T(8,128)(2,1)S(1)}, bf16[256,1792]{1,0:T(8,128)(2,1)}, u32[]{:S(2)}) copy-start(bf16[256,1792]{1,0:T(8,128)(2,1)} %gate_hbm.1) | copy-start | bytes 2752516
  94.2 4.0 %copy-start.2 = (bf16[4,32,1792]{2,1,0:T(8,128)(2,1)S(1)}, bf16[4,32,1792]{2,1,0:T(8,128)(2,1)}, u32[]{:S(2)}) copy-start(bf16[4,32,1792]{2,1,0:T(8,128)(2,1)} %get-tuple-element.8) | copy-start | bytes 1376260

commit v5 on v4

--- a/solution.py
+++ b/solution.py
@@ -32,9 +32,9 @@
 
 
 def kernel(
-    cot_hbm, gate_hbm, up_hbm, w_hbm, pt_hbm, acc_hbm, hx_hbm, rep_hbm,
-    wbuf, cotbuf, cot_own, pbuf, gate, up, hidden, acc, hx,
-    lr_part, lr_recv, low_rank, pg, ring_send, ring_recv, rep,
+    cot_hbm, gate_hbm, up_hbm, w_hbm, pt_hbm, gg_hbm, gu_hbm, rep_hbm,
+    wbuf, cotbuf, cot_own, pbuf, gate, up, act, factor, hidden, acc, hx, hx_in, gg, gu,
+    lr_full, lr_part, lr_recv, low_rank, pg, ring_send, ring_recv, rep,
     local_sem, out_sem, wz_s, wz_r, ws_s, ws_r, p_s, p_r, sib_s, sib_r,
     own_s, own_r, c_s, c_r, cr_s, cr_r, rs_s, rs_r, ag_s, ag_r, z_s, z_r, r_s, r_r, h_s, h_r,
 ):
@@ -171,6 +171,12 @@
         c_pair(0)
         c_whole(yl, 0, 0)
 
+    def c_mates():
+        c_mate(0).wait_recv()
+        c_mate(1).wait_recv()
+        c_pair(1)
+        c_whole(yl, 1, 0)
+
     def w_piece(way, m, zz):
         d, i = MESSAGES[m]
         at, size = (i * ROWS, ROWS) if d < 4 else (i * ROWS + way * 128, 128)
@@ -197,7 +203,7 @@
         ref = w_piece(way, m, z - sign * MESSAGES[m][0])
         return remote(ref, ref, ws_s.at[way, m], ws_r.at[way, m], sibling)
 
-    state = {"sent": 0, "event": 0, "ready": False, "todo": []}
+    state = {"sent": 0, "event": 0, "ready": False, "todo": [], "whole": False, "own": []}
 
     def w_push(done, lag):
         while state["sent"] < min(NM, done + 1 + lag) and needs(state["sent"]) <= done:
@@ -217,7 +223,11 @@
         if d == 4:
             state["todo"].append(i)
 
-    def compute(i, core):
+    def part(j, i):
+        cols = pl.ds(i * ROWS, ROWS)
+        return nt_dot(cotbuf[pl.ds(j * ROWS, ROWS), :], wbuf[cols, :])
+
+    def mates(i, core):
         if core == 1:
             w_own(i, 0).wait_recv()
             for m, (_, ii) in enumerate(MESSAGES):
@@ -225,29 +235,48 @@
                     w_pass(0, m).wait_recv()
                     w_pass(1, m).wait_recv()
         cols = pl.ds(i * ROWS, ROWS)
-
-        def part(j):
-            return nt_dot(cotbuf[pl.ds(j * ROWS, ROWS), :], wbuf[cols, :])
-
-        hx[:, cols] = part(1).astype(BF16)
-        acc[:, cols] = part(0)
-        start(remote(hx.at[:, cols], hx_hbm.at[:, cols], h_s.at[i], h_r.at[i], mate))
-        out = pltpu.make_async_copy(acc.at[:, cols], acc_hbm.at[:, cols], out_sem.at[i])
-        out.start()
-        outs.append(out)
+        hx[:, cols] = part(1, i).astype(BF16)
+        start(remote(hx.at[:, cols], hx_in.at[:, cols], h_s.at[i], h_r.at[i], mate))
+
+    def own(i):
+        acc[:, pl.ds(i * ROWS, ROWS)] = part(0, i)
+
+    def gradients(i):
+        cols = pl.ds(i * ROWS, ROWS)
+        remote(hx.at[:, cols], hx_in.at[:, cols], h_s.at[i], h_r.at[i], mate).wait_recv()
+        total = acc[:, cols] + hx_in[:, cols].astype(F32)
+        gg[:, cols] = (total * factor[:, cols]).astype(BF16)
+        gu[:, cols] = (total * act[:, cols]).astype(BF16)
+        for n, (here, there) in enumerate(((gg, gg_hbm), (gu, gu_hbm))):
+            out = pltpu.make_async_copy(
+                here.at[:, cols], there.at[:, cols], out_sem.at[2 * i + n]
+            )
+            out.start()
+            outs.append(out)
 
     def pump(events, lag=LAG):
         for _ in range(events):
             if state["event"] < NM:
                 w_event(lag)
             if state["ready"] and state["todo"]:
-                compute(state["todo"].pop(0), 0)
+                i = state["todo"].pop(0)
+                mates(i, 0)
+                state["own"].append(i)
+            elif state["whole"] and state["own"]:
+                i = state["own"].pop(0)
+                own(i)
+                if i > 1:
+                    gradients(i - 2)
 
     def make_hidden(i, carry):
         rows = pl.ds(pl.multiple_of(i * 16, 16), 16)
         g = gate[rows, :].astype(F32)
-        activated = g * jax.nn.sigmoid(g)
-        hidden[c, rows, :] = (activated * up[rows, :].astype(F32)).astype(BF16)
+        u = up[rows, :].astype(F32)
+        sigma = jax.nn.sigmoid(g)
+        activated = g * sigma
+        act[rows, :] = activated
+        factor[rows, :] = u * sigma * (1.0 + g * (1.0 - sigma))
+        hidden[c, rows, :] = (activated * u).astype(BF16)
         return carry
 
     def hidden_now():
@@ -265,7 +294,9 @@
         p_copy(0, 0, z).wait_recv()
         to_second(cot_own.at[0], 0).wait_recv()
         part = nt_dot(pbuf[...], cot_own[...].reshape(2 * ROWS, 512))
-        lr_part[...] = part.reshape(NT, 64, 2 * ROWS)
+        part = part.reshape(NT, 64, 2 * ROWS)
+        lr_full[...] = part
+        lr_part[...] = part.astype(BF16)
 
     def low_rank_scatter():
         for k in range(1, NT):
@@ -276,12 +307,12 @@
             ))
 
     def low_rank_sum():
-        total = lr_part[t]
+        total = lr_full[t]
         for k in range(1, NT):
             remote(
                 lr_part.at[t], lr_recv.at[k - 1], rs_s.at[k - 1], rs_r.at[k - 1], pair
             ).wait_recv()
-            total = total + lr_recv[k - 1]
+            total = total + lr_recv[k - 1].astype(F32)
         low_rank[t] = total.astype(BF16)
 
     def low_rank_gather():
@@ -341,7 +372,7 @@
             for core in (0, 1):
                 mine = rep.at[h, pl.ds(core * 32, 32), :]
                 if (k, core) == (0, 1):
-                    out = pltpu.make_async_copy(mine, there, out_sem.at[STREAMS + h])
+                    out = pltpu.make_async_copy(mine, there, out_sem.at[2 * STREAMS + h])
                     out.start()
                     outs.append(out)
                 else:
@@ -351,11 +382,8 @@
                     ))
 
     def finish(core):
-        for i in range(STREAMS):
-            cols = pl.ds(i * ROWS, ROWS)
-            remote(
-                hx.at[:, cols], hx_hbm.at[:, cols], h_s.at[i], h_r.at[i], mate
-            ).wait_recv()
+        for i in range(STREAMS - 2, STREAMS):
+            gradients(i)
         for h in (0, 1):
             for k in range(core, NR):
                 back = lax.rem(r - k + NR, NR)
@@ -373,39 +401,36 @@
     @pl.when(c == 0)
     def _():
         p_send(0)
-        loads[1].wait()
-        w_push(-1, LAG)
         c_begin()
         start(to_second(cot_own.at[0], 0))
+        loads[1].wait()
         for i in range(STREAMS):
             start(w_own(i, 0))
         hidden_now()
         start(to_second(hidden.at[0], 1))
+        w_push(-1, LAG)
+        c_mates()
+        pump(1)
+        c_pair_wait(1)
+        c_whole(1 - yl, 1, 1)
+        c_forward(yl, 1, 0)
+        pump(3)
+        c_forward(1 - yl, 1, 1)
+        pump(3)
+        c_last(yl, 1, 0)
+        c_last(1 - yl, 1, 1)
+        state["ready"] = True
         c_pair_wait(0)
         c_whole(1 - yl, 0, 1)
         c_forward(yl, 0, 0)
-        pump(1)
-        c_mate(0).wait_recv()
-        c_mate(1).wait_recv()
-        c_pair(1)
-        c_whole(yl, 1, 0)
-        pump(1)
+        pump(4)
         c_forward(1 - yl, 0, 1)
-        pump(2)
-        c_pair_wait(1)
-        c_whole(1 - yl, 1, 1)
-        c_forward(yl, 1, 0)
         pump(4)
-        c_forward(1 - yl, 1, 1)
-        pump(2)
         c_last(yl, 0, 0)
         c_last(1 - yl, 0, 1)
-        c_last(yl, 1, 0)
-        c_last(1 - yl, 1, 1)
-        state["ready"] = True
+        state["whole"] = True
         pump(NM)
-        for i in state["todo"]:
-            compute(i, 0)
+        assert not state["todo"] and not state["own"]
         finish(0)
 
     @pl.when(c == 1)
@@ -416,45 +441,77 @@
         p_send(1)
         c_begin()
         hidden_now()
+        c_mates()
+        low_rank_part()
+        low_rank_scatter()
+        c_pair_wait(1)
+        c_whole(1 - yl, 1, 1)
+        c_forward(yl, 1, 0)
+        low_rank_sum()
+        low_rank_gather()
+        c_forward(1 - yl, 1, 1)
         c_pair_wait(0)
         c_whole(1 - yl, 0, 1)
         c_forward(yl, 0, 0)
-        low_rank_part()
-        low_rank_scatter()
-        c_mate(0).wait_recv()
-        c_mate(1).wait_recv()
-        c_pair(1)
-        c_whole(yl, 1, 0)
-        c_forward(1 - yl, 0, 1)
-        low_rank_sum()
-        low_rank_gather()
-        c_pair_wait(1)
-        c_whole(1 - yl, 1, 1)
-        c_forward(yl, 1, 0)
         low_rank_wait()
         to_second(hidden.at[0], 1).wait_recv()
         lax.fori_loop(0, FF // 256, grad_tile, 0)
         ring_step(0, 0)
         ring_step(0, 1)
-        c_forward(1 - yl, 1, 1)
+        c_last(yl, 1, 0)
+        c_last(1 - yl, 1, 1)
+        c_forward(1 - yl, 0, 1)
+        mates(0, 1)
         ring_step(1, 0)
         ring_step(1, 1)
         c_last(yl, 0, 0)
         c_last(1 - yl, 0, 1)
-        c_last(yl, 1, 0)
-        c_last(1 - yl, 1, 1)
-        compute(0, 1)
+        own(0)
         ring_step(2, 0)
         ring_step(2, 1)
-        compute(1, 1)
+        mates(1, 1)
         ring_step(3, 0)
         ring_step(3, 1)
-        compute(2, 1)
+        mates(2, 1)
         replica_send(0)
         replica_send(1)
+        own(1)
         for i in range(3, STREAMS):
-            compute(i, 1)
+            mates(i, 1)
+            own(i - 1)
+            gradients(i - 3)
+        own(STREAMS - 1)
+        gradients(STREAMS - 3)
         finish(1)
+
+
+def tail(scale, gg_in, gu_in, parts_in, gg, gu, pg, gg_v, gu_v, parts_v, pg_v, sems):
+    quarters = []
+    for n, (here, buffer, there) in enumerate(((gg_in, gg_v, gg), (gu_in, gu_v, gu))):
+        for q in range(4):
+            rows = pl.ds(q * 64, 64)
+            i = n * 4 + q
+            quarters.append((
+                pltpu.make_async_copy(here.at[rows], buffer.at[rows], sems.at[0, i]),
+                pltpu.make_async_copy(buffer.at[rows], there.at[rows], sems.at[1, i]),
+            ))
+    parts = pltpu.make_async_copy(parts_in, parts_v, sems.at[0, 8])
+    result = pltpu.make_async_copy(pg_v, pg, sems.at[1, 8])
+    parts.start()
+    for load, _ in quarters:
+        load.start()
+    parts.wait()
+    total = parts_v[0].astype(F32)
+    for k in range(1, NR):
+        total = total + parts_v[k].astype(F32)
+    pg_v[...] = total * scale
+    result.start()
+    for load, store in quarters:
+        load.wait()
+        store.start()
+    for _, store in quarters:
+        store.wait()
+    result.wait()
 
 
 def local(cotangent, gate_pre, up_pre, down_weight, projector):
@@ -464,10 +521,10 @@
     scale = 1.0 / math.sqrt(tokens)
     dma = pltpu.SemaphoreType.DMA
     hbm = pl.BlockSpec(memory_space=pl.ANY)
-    own, other, parts = pl.pallas_call(
+    grad_gate, grad_up, parts = pl.pallas_call(
         kernel,
         out_shape=(
-            jax.ShapeDtypeStruct((rows, ff), F32),
+            jax.ShapeDtypeStruct((rows, ff), BF16),
             jax.ShapeDtypeStruct((rows, ff), BF16),
             jax.ShapeDtypeStruct((NR, 32, ff), BF16),
         ),
@@ -480,17 +537,23 @@
             pltpu.VMEM((512, width), BF16),
             pltpu.VMEM((rows, ff), BF16),
             pltpu.VMEM((rows, ff), BF16),
+            pltpu.VMEM((rows, ff), F32),
+            pltpu.VMEM((rows, ff), F32),
             pltpu.VMEM((2, rows, ff), BF16),
             pltpu.VMEM((rows, ff), F32),
             pltpu.VMEM((rows, ff), BF16),
+            pltpu.VMEM((rows, ff), BF16),
+            pltpu.VMEM((rows, ff), BF16),
+            pltpu.VMEM((rows, ff), BF16),
             pltpu.VMEM((NT, 64, 2 * rows), F32),
-            pltpu.VMEM((NT - 1, 64, 2 * rows), F32),
+            pltpu.VMEM((NT, 64, 2 * rows), BF16),
+            pltpu.VMEM((NT - 1, 64, 2 * rows), BF16),
             pltpu.VMEM((NT, 64, 2 * rows), BF16),
             pltpu.VMEM((NZ, 64, ff), F32),
             pltpu.VMEM((2, 7, 64, HALF), BF16),
             pltpu.VMEM((2, 7, 64, HALF), BF16),
             pltpu.VMEM((2, 64, HALF), BF16),
-            dma((7,)), dma((STREAMS + 2,)),
+            dma((7,)), dma((2 * STREAMS + 2,)),
             dma((2, NM)), dma((2, NM)), dma((2, NM)), dma((2, NM)),
             dma((2, NZ)), dma((2, NZ)), dma((2,)), dma((2,)),
             dma((2, STREAMS)), dma((2, STREAMS)),
@@ -505,14 +568,24 @@
         name="mlp_backward",
     )(cotangent, gate_pre, up_pre, down_weight, projector.T)
 
-    hidden_grad = own + other.astype(F32)
-    gate_float = gate_pre.astype(F32)
-    up_float = up_pre.astype(F32)
-    sigma = jax.nn.sigmoid(gate_float)
-    grad_up = (hidden_grad * (gate_float * sigma)).astype(BF16)
-    grad_gate = (hidden_grad * up_float * sigma * (1.0 + gate_float * (1.0 - sigma))).astype(BF16)
-    projected_grad = jnp.sum(parts.astype(F32), axis=0) * scale
-    return (grad_gate, grad_up, projected_grad)
+    return pl.pallas_call(
+        functools.partial(tail, scale),
+        out_shape=(
+            jax.ShapeDtypeStruct((rows, ff), BF16),
+            jax.ShapeDtypeStruct((rows, ff), BF16),
+            jax.ShapeDtypeStruct((32, ff), F32),
+        ),
+        in_specs=[hbm] * 3,
+        out_specs=(hbm,) * 3,
+        scratch_shapes=[
+            pltpu.VMEM((rows, ff), BF16),
+            pltpu.VMEM((rows, ff), BF16),
+            pltpu.VMEM((NR, 32, ff), BF16),
+            pltpu.VMEM((32, ff), F32),
+            dma((2, 9)),
+        ],
+        name="outputs",
+    )(grad_gate, grad_up, parts)
 
 
 def solution(mesh):

time: 99.7 us -> 94.9 us (0.952)
  other arithmetic: 4.79 us -> 0 us
    convert_element_type x1 -> x0, other arithmetic: 4.02 us -> none  [local(): grad_up = (hidden_grad * (gate_float * sigma)).astype(BF16)]
    pallas_call x1 -> x2, Pallas kernels: 93.6 us -> 92.9 us  [the longest x1 90.3 us: local(): pl.pallas_call(kernel, out_shape=(jax.ShapeDtypeStruct((rows, ff), BF16),...]
where the time goes in v5:
time: 94.9 us; the launch traced here: 93.7 us
  Pallas kernels  92.9 us (98%)
    pallas_call x1, Pallas kernels, local(): pl.pallas_call(kernel, out_shape=(jax.ShapeDtypeStruct((rows, ff), BF16),...  90.3 us
    pallas_call x1, Pallas kernels, local(): pl.pallas_call(functools.partial(tail, scale), out_shape=(jax.ShapeDtypeS...  2.53 us

profile of v5, /device:TPU:1, one launch (start us, length us, event | category | flops | bytes accessed | tf_op | source)
XLA Modules:
  0.0 93.7 jit_solution(13110899090239751584)
XLA Ops:
  0.6 90.3 %mlp_backward.1 = (bf16[256,1792]{1,0:T(8,128)(2,1)}, bf16[256,1792]{1,0:T(8,128)(2,1)}, bf16[4,32,1792]{2,1,0:T(8,128)(2,1)}) custom-call(bf16[256,512]{1,0:T(8,128)(2,1)} %cot_hbm.1, bf16[256,1792]{1,0:T(8,128)(2,1)} %gate_hbm.1, bf16[256,1792]{1,0:T(8,128)(2,1)} %up_hbm.1, bf16[1792,256]{1,0:T(8,128)(2,1)} %w_hbm.1, bf16[32,512]{1,0:T(8,128)(2,1)} %bitcast.1), custom_call_target="tpu_custom_call" | custom-call | tf_op jit(solution)/shard_map/mlp_backward/pallas_call | solution.py:524
  91.0 2.5 %outputs.1 = (bf16[256,1792]{1,0:T(8,128)(2,1)}, bf16[256,1792]{1,0:T(8,128)(2,1)}, f32[32,1792]{1,0:T(8,128)}) custom-call(bf16[256,1792]{1,0:T(8,128)(2,1)} %get-tuple-element.6.gg_in, bf16[256,1792]{1,0:T(8,128)(2,1)} %get-tuple-element.7.gu_in, bf16[4,32,1792]{2,1,0:T(8,128)(2,1)} %get-tuple-element.8.parts_in), custom_call_target="tpu_custom_call" | custom-call | tf_op jit(solution)/shard_map/outputs/pallas_call | solution.py:571

commit v6 on v5

--- a/solution.py
+++ b/solution.py
@@ -24,7 +24,6 @@
     key=lambda m: (2 * m[1] + 3 * m[0], m[1]),
 )
 NM = len(MESSAGES)
-NEAR_FIRST = (1, 7, 2, 6, 3, 5, 4)
 
 
 def nt_dot(a, b):
@@ -109,16 +108,22 @@
         )
     pl.semaphore_wait(barrier, len(greet))
 
-    def p_copy(core, k, zz):
-        ref = pbuf.at[rows_at((zz * 2 + core) * 32, 32), :]
-        return remote(ref, ref, p_s.at[core, k], p_r.at[core, k], zdev(k, 1))
-
-    def p_send(core):
-        loads[0].wait()
-        for k in NEAR_FIRST:
-            start(p_copy(core, k, z))
-        if core == 0:
-            start(p_copy(core, 0, z))
+    def p_pass(core_rows, size, device, way, d):
+        ref = pbuf.at[rows_at(core_rows, size), :]
+        return remote(ref, ref, p_s.at[way, d], p_r.at[way, d], device)
+
+    def p_hop(way, d, behind):
+        sign = 1 - 2 * way
+        at = lax.rem(z - sign * behind + NZ, NZ)
+        return p_pass(at * 64, 64, zdev(sign), way, d)
+
+    def p_relay(d):
+        for way in (0, 1):
+            if d <= 4 - way:
+                if d > 0:
+                    p_hop(way, d, d).wait_recv()
+                if d + 1 <= 4 - way:
+                    start(p_hop(way, d + 1, d))
 
     def chunk(row, xx, j, part=None):
         at = row * NX + lax.rem(xx + NX, NX)
@@ -288,10 +293,6 @@
         return remote(ref, ref, sib_s.at[i], sib_r.at[i], sibling)
 
     def low_rank_part():
-        for k in NEAR_FIRST:
-            p_copy(0, k, lax.rem(z - k + NZ, NZ)).wait_recv()
-            p_copy(1, k, lax.rem(z - k + NZ, NZ)).wait_recv()
-        p_copy(0, 0, z).wait_recv()
         to_second(cot_own.at[0], 0).wait_recv()
         part = nt_dot(pbuf[...], cot_own[...].reshape(2 * ROWS, 512))
         part = part.reshape(NT, 64, 2 * ROWS)
@@ -341,18 +342,21 @@
     def own_part(zz, h):
         return pg[lax.rem(zz + NZ, NZ), :, pl.ds(h * HALF, HALF)]
 
+    def turn(way, h):
+        return (1 - 2 * way) * (1 - 2 * h)
+
     def ring(way, step, h):
         i = way * 4 + step
         return remote(
             ring_send.at[h, i], ring_recv.at[h, i], z_s.at[h, i], z_r.at[h, i],
-            zdev(1 - 2 * way),
+            zdev(turn(way, h)),
         )
 
     def ring_step(step, h):
         for way in (0, 1):
             if step < 4 - way:
                 i = way * 4 + step
-                value = own_part(z + (1 - 2 * way) * (4 - way - step), h)
+                value = own_part(z + turn(way, h) * (4 - way - step), h)
                 if step > 0:
                     ring(way, step - 1, h).wait_recv()
                     value = value + ring_recv[h, i - 1].astype(F32)
@@ -400,7 +404,8 @@
 
     @pl.when(c == 0)
     def _():
-        p_send(0)
+        loads[0].wait()
+        start(p_pass(z * 64, 32, sibling, 0, 0))
         c_begin()
         start(to_second(cot_own.at[0], 0))
         loads[1].wait()
@@ -438,14 +443,20 @@
         loads[1].wait()
         for i in range(STREAMS):
             start(w_own(i, 1))
-        p_send(1)
+        loads[0].wait()
+        p_pass(z * 64, 32, sibling, 0, 0).wait_recv()
+        p_relay(0)
         c_begin()
-        hidden_now()
+        p_relay(1)
+        p_relay(2)
         c_mates()
+        p_relay(3)
+        p_relay(4)
         low_rank_part()
         low_rank_scatter()
         c_pair_wait(1)
         c_whole(1 - yl, 1, 1)
+        hidden_now()
         c_forward(yl, 1, 0)
         low_rank_sum()
         low_rank_gather()

time: 94.9 us -> 95.2 us (level)
  Pallas kernels: 92.9 us -> 94 us
    pallas_call x1, Pallas kernels: 90.3 us -> 91.5 us  [local(): pl.pallas_call(kernel, out_shape=(jax.ShapeDtypeStruct((rows, ff), BF16),...]
where the time goes in v6:
time: 95.2 us; the launch traced here: 94.8 us
  Pallas kernels  94 us (99%)
    pallas_call x1, Pallas kernels, local(): pl.pallas_call(kernel, out_shape=(jax.ShapeDtypeStruct((rows, ff), BF16),...  91.5 us
    pallas_call x1, Pallas kernels, local(): pl.pallas_call(functools.partial(tail, scale), out_shape=(jax.ShapeDtypeS...  2.53 us

profile of v6, /device:TPU:1, one launch (start us, length us, event | category | flops | bytes accessed | tf_op | source)
XLA Modules:
  0.0 94.8 jit_solution(9114994570080912488)
XLA Ops:
  0.6 91.5 %mlp_backward.1 = (bf16[256,1792]{1,0:T(8,128)(2,1)}, bf16[256,1792]{1,0:T(8,128)(2,1)}, bf16[4,32,1792]{2,1,0:T(8,128)(2,1)}) custom-call(bf16[256,512]{1,0:T(8,128)(2,1)} %cot_hbm.1, bf16[256,1792]{1,0:T(8,128)(2,1)} %gate_hbm.1, bf16[256,1792]{1,0:T(8,128)(2,1)} %up_hbm.1, bf16[1792,256]{1,0:T(8,128)(2,1)} %w_hbm.1, bf16[32,512]{1,0:T(8,128)(2,1)} %bitcast.1), custom_call_target="tpu_custom_call" | custom-call | tf_op jit(solution)/shard_map/mlp_backward/pallas_call | solution.py:535
  92.1 2.5 %outputs.1 = (bf16[256,1792]{1,0:T(8,128)(2,1)}, bf16[256,1792]{1,0:T(8,128)(2,1)}, f32[32,1792]{1,0:T(8,128)}) custom-call(bf16[256,1792]{1,0:T(8,128)(2,1)} %get-tuple-element.6.gg_in, bf16[256,1792]{1,0:T(8,128)(2,1)} %get-tuple-element.7.gu_in, bf16[4,32,1792]{2,1,0:T(8,128)(2,1)} %get-tuple-element.8.parts_in), custom_call_target="tpu_custom_call" | custom-call | tf_op jit(solution)/shard_map/outputs/pallas_call | solution.py:582
